TPU v7x, 768 devices: a whole 4x8x12 slice. The times are simulated.
768 devices in a mesh: grp: 192 (over x, y_lo, z), tp: 4 (over y_hi, core).
Axes of the slice: x: 4, y: 8 (y_hi: 2, y_lo: 4; y = y_hi * 4 + y_lo), z: 12, core: 2. Of those that a mesh axis runs over, the one named last changes fastest.
Arguments:
- activations: bfloat16 [49152, 5120], P('grp', 'tp'), may hold values from -6 to 6
- cotangent: bfloat16 [49152, 512], P('grp'), may hold values from -1.5 to 1.5
- advantage: int32 [192], replicated, may hold values from -512 to 512
- seq_len: int32 [192], replicated, may hold values from 64 to 256, as said below
- key_master: float32 [4, 1344, 512], P('tp', 'grp'), may hold values from -0.078125 to 0.078125
- moment_one: float32 [4, 1344, 512], P('tp', 'grp'), may hold values from -3 to 3
- moment_two: float32 [4, 1344, 512], P('tp', 'grp'), may hold values from 0.1 to 2
- decode_hidden: bfloat16 [192, 4, 5120], P('grp'), may hold values from -6 to 6
- queries: bfloat16 [192, 4, 2560], P('grp', None, 'tp'), may hold values from -34 to 34
- cache_keys: bfloat16 [192, 2048, 512], P('grp', None, 'tp'), may hold values from -6 to 6
- cache_values: bfloat16 [192, 2048, 512], P('grp', None, 'tp'), may hold values from -6 to 6
- cache_len: int32 [192], P('grp'), may hold values from 2 to 2048, as said below
- value_weight: bfloat16 [5120, 512], P(None, 'tp'), may hold values from -0.078125 to 0.078125
Outputs:
- master_new: float32 [4, 1344, 512], P('tp', 'grp')
- moment_one_new: float32 [4, 1344, 512], P('tp', 'grp')
- moment_two_new: float32 [4, 1344, 512], P('tp', 'grp')
- new_keys: bfloat16 [192, 4, 512], P('grp', None, 'tp')
- new_values: bfloat16 [192, 4, 512], P('grp', None, 'tp')
- attention: bfloat16 [192, 4, 2560], P('grp', None, 'tp')
Inputs may be any that keep to these rules, and one draw needn't show every extreme that they name: `seq_len`: the first sequence is full. `cache_len`: row 0 has a full cache.
All inputs are finite; a program needn't handle non-finite values.
Results may differ from a plain program's by a relative error of at most 0.0044.
The roundings to bfloat16 on the way count: a program that leaves them out, or rounds other values in their place, can miss the bound.
Values may be sent and summed in bfloat16 or wider, within the bound.
No kernel may reach another device: no remote copies, remote signals or barrier semaphores. Data moves between devices by JAX's collectives and lax.ppermute only.
A program may use at most 32 MiB of HBM per device.

v0:
```python
import math

import jax
import jax.numpy as jnp
from jax import lax
from jax.sharding import PartitionSpec as P

HD = 128
GQA = 5
SEQ = 256


def attend(queries, cache_keys, cache_values, cache_len, new_keys, new_values):
    rows, steps, width = queries.shape
    length = cache_keys.shape[1]
    heads_kv = cache_keys.shape[2] // HD
    inverse = 1.0 / math.sqrt(HD)
    shaped_q = queries.reshape(rows, steps, heads_kv, GQA, HD)
    keys_c = cache_keys.reshape(rows, length, heads_kv, HD)
    vals_c = cache_values.reshape(rows, length, heads_kv, HD)
    keys_n = new_keys.reshape(rows, steps, heads_kv, HD)
    vals_n = new_values.reshape(rows, steps, heads_kv, HD)
    score_c = (
        jnp.einsum("rsgqd,rcgd->rgsqc", shaped_q, keys_c, preferred_element_type=jnp.float32)
        * inverse
    )
    score_n = (
        jnp.einsum("rsgqd,rtgd->rgsqt", shaped_q, keys_n, preferred_element_type=jnp.float32)
        * inverse
    )
    valid = jnp.arange(length, dtype=jnp.int32)[None, :] < cache_len[:, None]
    score_c = jnp.where(valid[:, None, None, None, :], score_c, -jnp.inf)
    causal = (
        jnp.arange(steps, dtype=jnp.int32)[None, :] <= jnp.arange(steps, dtype=jnp.int32)[:, None]
    )
    score_n = jnp.where(causal[None, None, :, None, :], score_n, -jnp.inf)
    top = jnp.maximum(jnp.max(score_c, axis=-1), jnp.max(score_n, axis=-1))
    exp_c = jnp.exp(score_c - top[..., None])
    exp_n = jnp.exp(score_n - top[..., None])
    total = jnp.sum(exp_c, axis=-1) + jnp.sum(exp_n, axis=-1)
    probs_c = (exp_c / total[..., None]).astype(jnp.bfloat16)
    probs_n = (exp_n / total[..., None]).astype(jnp.bfloat16)
    mixed = jnp.einsum("rgsqc,rcgd->rsgqd", probs_c, vals_c, preferred_element_type=jnp.float32)
    mixed = mixed + jnp.einsum(
        "rgsqt,rtgd->rsgqd", probs_n, vals_n, preferred_element_type=jnp.float32
    )
    return mixed.astype(jnp.bfloat16).reshape(rows, steps, width)


def shards(
    activations,
    cotangent,
    advantage,
    seq_len,
    key_master,
    moment_one,
    moment_two,
    decode_hidden,
    queries,
    cache_keys,
    cache_values,
    cache_len,
    value_weight,
):
    tok_rows = activations.shape[0]
    quarter_rows = activations.shape[1]
    groups = lax.axis_size("grp")
    sequences = seq_len.shape[0]
    position = lax.axis_index("grp") * tok_rows + jnp.arange(tok_rows, dtype=jnp.int32)
    seq_index = position // SEQ
    within = position % SEQ
    onehot = seq_index[:, None] == jnp.arange(sequences, dtype=jnp.int32)[None, :]
    length_tok = jnp.sum(jnp.where(onehot, seq_len[None, :], 0), axis=1)
    adv_tok = jnp.sum(jnp.where(onehot, advantage[None, :], 0), axis=1).astype(jnp.float32) / 256.0
    scale = jnp.where(within < length_tok, adv_tok, jnp.float32(0.0)) / sequences
    weighted = (cotangent.astype(jnp.float32) * scale[:, None]).astype(jnp.bfloat16)
    own_rows = key_master.shape[1]
    padded = jnp.pad(activations, ((0, 0), (0, own_rows * groups - quarter_rows)))
    gradient = lax.psum_scatter(
        lax.dot_general(
            padded, weighted, (((0,), (0,)), ((), ())), preferred_element_type=jnp.float32
        ),
        "grp",
        scatter_dimension=0,
        tiled=True,
    )
    gradient = gradient.reshape(key_master.shape)
    corr_one = 1.0 - 0.9**10
    corr_two = 1.0 - 0.95**10
    moment_one_new = 0.9 * moment_one + 0.1 * gradient
    moment_two_new = 0.95 * moment_two + 0.05 * gradient * gradient
    master_new = key_master - 0.005 * (moment_one_new / corr_one) / (
        jnp.sqrt(moment_two_new / corr_two) + 1e-08
    )
    relay = master_new.astype(jnp.bfloat16)
    quarter = lax.all_gather(relay, "grp", axis=1, tiled=True)
    quarter = quarter[0, :quarter_rows]
    weight_cols = lax.all_to_all(quarter, "tp", split_axis=1, concat_axis=0, tiled=True)
    rows, steps, width = decode_hidden.shape
    flat_hidden = decode_hidden.reshape(rows * steps, width)
    new_keys = (
        jnp.dot(flat_hidden, weight_cols, preferred_element_type=jnp.float32)
        .astype(jnp.bfloat16)
        .reshape(rows, steps, -1)
    )
    new_values = (
        jnp.dot(flat_hidden, value_weight, preferred_element_type=jnp.float32)
        .astype(jnp.bfloat16)
        .reshape(rows, steps, -1)
    )
    attention = attend(queries, cache_keys, cache_values, cache_len, new_keys, new_values)
    return (master_new, moment_one_new, moment_two_new, new_keys, new_values, attention)


def solution(mesh):
    placed = (
        P("grp", "tp"),
        P("grp", None),
        P(),
        P(),
        P("tp", "grp", None),
        P("tp", "grp", None),
        P("tp", "grp", None),
        P("grp", None, None),
        P("grp", None, "tp"),
        P("grp", None, "tp"),
        P("grp", None, "tp"),
        P("grp"),
        P(None, "tp"),
    )
    return jax.shard_map(
        shards,
        mesh=mesh,
        in_specs=placed,
        out_specs=(
            P("tp", "grp", None),
            P("tp", "grp", None),
            P("tp", "grp", None),
            P("grp", None, "tp"),
            P("grp", None, "tp"),
            P("grp", None, "tp"),
        ),
        check_vma=False,
    )
```

profile of v0, /device:TPU:1, one launch (start us, length us, event | category | flops | bytes accessed | tf_op | source)
XLA Modules:
  0.0 1771.4 jit_solution(6345067619892343134)
XLA Ops:
  8.2 3.3 fusion.6
  11.5 490.2 %fusion = f32[8,512]{1,0:T(8,128)S(1)} fusion(f32[1344,512]{1,0:T(8,128)} %fusion.6), kind=kCustom, calls=%all-reduce-scatter | all-reduce-scatter fusion | flops 786433 | bytes 2772992
  514.8 32.3 %collective-permute-start.13 = (f32[8,512]{1,0:T(8,128)S(1)}, f32[8,512]{1,0:T(8,128)S(1)}, u32[]{:S(2)}, u32[]{:S(2)}) collective-permute-start(f32[8,512]{1,0:T(8,128)S(1)} %fusion), channel_id=1, source_target_pairs={{0,56},{4,60},{8,64},{12,68},{16,72},{20,76},{24,80},{28,84},{32,8... | collective-permute-start | bytes 49160
  547.1 2.5 collective-permute-start.12
  549.6 4.9 collective-permute-start.11
  554.5 3.1 collective-permute-start.10
  557.7 2.8 collective-permute-start.9
  560.5 4.0 collective-permute-start.8
  564.5 6.7 collective-permute-start.7
  571.3 3.4 collective-permute-start.6
  574.6 7.1 collective-permute-start.5
  581.7 2.8 collective-permute-start.4
  584.5 5.8 collective-permute-start.3
  590.3 4.0 collective-permute-start.2
  594.3 1.9 collective-permute-start.1
  596.3 2.8 collective-permute-start
  601.1 2.4 concatenate
  604.2 977.9 %all-gather.2.cloned.1.call-done = bf16[1,1344,512]{2,0,1:T(2,128)(2,1)} async-done(((bf16[1,7,512]{2,0,1:T(2,128)(2,1)}), bf16[1,1344,512]{2,0,1:T(2,128)(2,1)}) %all-gather.2.cloned.1.call-update) | async-done | bytes 1376272 | tf_op jit(solution)/shard_map/all_gather | solution.py:96
  1582.0 6.0 slice.4
  1588.0 6.1 copy.57
  1594.1 145.6 %all-to-all-start = ((bf16[1280,4,128]{0,2,1:T(8,128)(2,1)}), bf16[1280,4,128]{0,2,1:T(8,128)(2,1)S(1)}, u32[]{:S(2)}, u32[]{:S(2)}) async-start(bf16[1280,4,128]{0,2,1:T(8,128)(2,1)} %bitcast.61), calls=%async_computation | async-start | bytes 2621440 | tf_op jit(solution)/shard_map/all_to_all | solution.py:98
  1742.9 17.0 all-to-all-done
  1759.9 1.4 copy.53
  1761.4 1.6 convolution_convert_fusion.1
  (79 shorter events, 19.9 us)
Async XLA Ops:
  7.2 1574.8 %all-gather.2.cloned.1.call-start = ((), (), s32[]{:S(2)}) async-start(), calls=%async_computation.1 | async-start | bytes 2766848 | tf_op jit(solution)/shard_map/all_gather | solution.py:96
  501.7 7.8 collective-permute-start.22
  503.0 7.8 collective-permute-start.21
  504.3 7.8 collective-permute-start.20
  506.9 6.5 collective-permute-start.19
  508.2 6.5 collective-permute-start.18
  509.5 37.5 %collective-permute-start.17 = (f32[8,512]{1,0:T(8,128)S(1)}, f32[8,512]{1,0:T(8,128)S(1)}, u32[]{:S(2)}, u32[]{:S(2)}) collective-permute-start(f32[8,512]{1,0:T(8,128)S(1)} %fusion), channel_id=1, source_target_pairs={{0,72},{4,76},{8,80},{12,84},{16,88},{20,92},{24,96},{28,100},{32,... | collective-permute-start | bytes 49160
  510.8 38.8 %collective-permute-start.16 = (f32[8,512]{1,0:T(8,128)S(1)}, f32[8,512]{1,0:T(8,128)S(1)}, u32[]{:S(2)}, u32[]{:S(2)}) collective-permute-start(f32[8,512]{1,0:T(8,128)S(1)} %fusion), channel_id=1, source_target_pairs={{0,68},{4,72},{8,76},{12,80},{16,84},{20,88},{24,92},{28,96},{32,1... | collective-permute-start | bytes 49160
  512.2 42.4 %collective-permute-start.15 = (f32[8,512]{1,0:T(8,128)S(1)}, f32[8,512]{1,0:T(8,128)S(1)}, u32[]{:S(2)}, u32[]{:S(2)}) collective-permute-start(f32[8,512]{1,0:T(8,128)S(1)} %fusion), channel_id=1, source_target_pairs={{0,64},{4,68},{8,72},{12,76},{16,80},{20,84},{24,88},{28,92},{32,9... | collective-permute-start | bytes 49160
  513.5 44.2 %collective-permute-start.14 = (f32[8,512]{1,0:T(8,128)S(1)}, f32[8,512]{1,0:T(8,128)S(1)}, u32[]{:S(2)}, u32[]{:S(2)}) collective-permute-start(f32[8,512]{1,0:T(8,128)S(1)} %fusion), channel_id=1, source_target_pairs={{0,60},{4,64},{8,68},{12,72},{16,76},{20,80},{24,84},{28,88},{32,9... | collective-permute-start | bytes 49160
  514.8 45.7 %collective-permute-start.13 = (f32[8,512]{1,0:T(8,128)S(1)}, f32[8,512]{1,0:T(8,128)S(1)}, u32[]{:S(2)}, u32[]{:S(2)}) collective-permute-start(f32[8,512]{1,0:T(8,128)S(1)} %fusion), channel_id=1, source_target_pairs={{0,56},{4,60},{8,64},{12,68},{16,72},{20,76},{24,80},{28,84},{32,8... | collective-permute-start | bytes 49160
  547.1 17.4 collective-permute-start.12
  549.6 21.6 %collective-permute-start.11 = (f32[8,512]{1,0:T(8,128)S(1)}, f32[8,512]{1,0:T(8,128)S(1)}, u32[]{:S(2)}, u32[]{:S(2)}) collective-permute-start(f32[8,512]{1,0:T(8,128)S(1)} %fusion), channel_id=1, source_target_pairs={{0,48},{4,52},{8,56},{12,60},{16,64},{20,68},{24,72},{28,76},{32,8... | collective-permute-start | bytes 49160
  554.5 20.1 %collective-permute-start.10 = (f32[8,512]{1,0:T(8,128)S(1)}, f32[8,512]{1,0:T(8,128)S(1)}, u32[]{:S(2)}, u32[]{:S(2)}) collective-permute-start(f32[8,512]{1,0:T(8,128)S(1)} %fusion), channel_id=1, source_target_pairs={{0,44},{4,48},{8,52},{12,56},{16,60},{20,64},{24,68},{28,72},{32,7... | collective-permute-start | bytes 49160
  557.7 24.0 %collective-permute-start.9 = (f32[8,512]{1,0:T(8,128)S(1)}, f32[8,512]{1,0:T(8,128)S(1)}, u32[]{:S(2)}, u32[]{:S(2)}) collective-permute-start(f32[8,512]{1,0:T(8,128)S(1)} %fusion), channel_id=1, source_target_pairs={{0,40},{4,44},{8,48},{12,52},{16,56},{20,60},{24,64},{28,68},{32,7... | collective-permute-start | bytes 49160
  560.5 24.0 %collective-permute-start.8 = (f32[8,512]{1,0:T(8,128)S(1)}, f32[8,512]{1,0:T(8,128)S(1)}, u32[]{:S(2)}, u32[]{:S(2)}) collective-permute-start(f32[8,512]{1,0:T(8,128)S(1)} %fusion), channel_id=1, source_target_pairs={{0,36},{4,40},{8,44},{12,48},{16,52},{20,56},{24,60},{28,64},{32,6... | collective-permute-start | bytes 49160
  564.5 25.8 %collective-permute-start.7 = (f32[8,512]{1,0:T(8,128)S(1)}, f32[8,512]{1,0:T(8,128)S(1)}, u32[]{:S(2)}, u32[]{:S(2)}) collective-permute-start(f32[8,512]{1,0:T(8,128)S(1)} %fusion), channel_id=1, source_target_pairs={{0,32},{4,36},{8,40},{12,44},{16,48},{20,52},{24,56},{28,60},{32,6... | collective-permute-start | bytes 49160
  571.3 23.1 %collective-permute-start.6 = (f32[8,512]{1,0:T(8,128)S(1)}, f32[8,512]{1,0:T(8,128)S(1)}, u32[]{:S(2)}, u32[]{:S(2)}) collective-permute-start(f32[8,512]{1,0:T(8,128)S(1)} %fusion), channel_id=1, source_target_pairs={{0,28},{4,32},{8,36},{12,40},{16,44},{20,48},{24,52},{28,56},{32,6... | collective-permute-start | bytes 49160
  574.6 21.6 %collective-permute-start.5 = (f32[8,512]{1,0:T(8,128)S(1)}, f32[8,512]{1,0:T(8,128)S(1)}, u32[]{:S(2)}, u32[]{:S(2)}) collective-permute-start(f32[8,512]{1,0:T(8,128)S(1)} %fusion), channel_id=1, source_target_pairs={{0,24},{4,28},{8,32},{12,36},{16,40},{20,44},{24,48},{28,52},{32,5... | collective-permute-start | bytes 49160
  581.7 19.3 %collective-permute-start.4 = (f32[8,512]{1,0:T(8,128)S(1)}, f32[8,512]{1,0:T(8,128)S(1)}, u32[]{:S(2)}, u32[]{:S(2)}) collective-permute-start(f32[8,512]{1,0:T(8,128)S(1)} %fusion), channel_id=1, source_target_pairs={{0,20},{4,24},{8,28},{12,32},{16,36},{20,40},{24,44},{28,48},{32,5... | collective-permute-start | bytes 49160
  584.5 16.5 collective-permute-start.3
  590.3 10.7 collective-permute-start.2
  594.3 6.7 collective-permute-start.1
  1594.1 165.8 %all-to-all-start = ((bf16[1280,4,128]{0,2,1:T(8,128)(2,1)}), bf16[1280,4,128]{0,2,1:T(8,128)(2,1)S(1)}, u32[]{:S(2)}, u32[]{:S(2)}) async-start(bf16[1280,4,128]{0,2,1:T(8,128)(2,1)} %bitcast.61), calls=%async_computation | async-start | bytes 2621440 | tf_op jit(solution)/shard_map/all_to_all | solution.py:98
  (12 other events, 3981.8 us)
Sparse Core Ops, SparseCore 0:
  604.3 977.6 all-gather.1
where the time goes:
time: 1770 us
  waiting for transfers between devices  995 us (56%)
  blocking collectives  490 us (28%)
  starting transfers between devices  243 us (14%)
  local copies, waits for them, and re-layouts  20.4 us (1%)
    all_gather x1, waiting for transfers between devices, shards(): quarter = lax.all_gather(relay, 'grp', axis=1, tiled=True)  978 us
    unnamed x1, blocking collectives  490 us
    all_to_all x1, starting transfers between devices, shards(): lax.all_to_all(quarter, 'tp', split_axis=1, concat_axis=0, tiled=True)  146 us
    unnamed x24, starting transfers between devices  97 us
  transfers between devices with their start and end apart: 26, of which 2 were waited for; matrix products, arithmetic and copies ran while one was open for 0% of the time, Pallas kernels for 0%

commit v1 on v0

v1 whole, which is shorter than its diff:
```python
import math

import jax
import jax.numpy as jnp
from jax import lax
from jax.sharding import Mesh, PartitionSpec as P

HD = 128
GQA = 5
SEQ = 256
NX, NY, NZ = 4, 4, 12
OWN = 7
PAD = 8
TP = 4


def attend(queries, cache_keys, cache_values, cache_len, new_keys, new_values):
    rows, steps, width = queries.shape
    length = cache_keys.shape[1]
    heads_kv = cache_keys.shape[2] // HD
    inverse = 1.0 / math.sqrt(HD)
    shaped_q = queries.reshape(rows, steps, heads_kv, GQA, HD)
    keys_c = cache_keys.reshape(rows, length, heads_kv, HD)
    vals_c = cache_values.reshape(rows, length, heads_kv, HD)
    keys_n = new_keys.reshape(rows, steps, heads_kv, HD)
    vals_n = new_values.reshape(rows, steps, heads_kv, HD)
    score_c = (
        jnp.einsum("rsgqd,rcgd->rgsqc", shaped_q, keys_c, preferred_element_type=jnp.float32)
        * inverse
    )
    score_n = (
        jnp.einsum("rsgqd,rtgd->rgsqt", shaped_q, keys_n, preferred_element_type=jnp.float32)
        * inverse
    )
    valid = jnp.arange(length, dtype=jnp.int32)[None, :] < cache_len[:, None]
    score_c = jnp.where(valid[:, None, None, None, :], score_c, -jnp.inf)
    causal = (
        jnp.arange(steps, dtype=jnp.int32)[None, :] <= jnp.arange(steps, dtype=jnp.int32)[:, None]
    )
    score_n = jnp.where(causal[None, None, :, None, :], score_n, -jnp.inf)
    top = jnp.maximum(jnp.max(score_c, axis=-1), jnp.max(score_n, axis=-1))
    exp_c = jnp.exp(score_c - top[..., None])
    exp_n = jnp.exp(score_n - top[..., None])
    total = jnp.sum(exp_c, axis=-1) + jnp.sum(exp_n, axis=-1)
    probs_c = (exp_c / total[..., None]).astype(jnp.bfloat16)
    probs_n = (exp_n / total[..., None]).astype(jnp.bfloat16)
    mixed = jnp.einsum("rgsqc,rcgd->rsgqd", probs_c, vals_c, preferred_element_type=jnp.float32)
    mixed = mixed + jnp.einsum(
        "rgsqt,rtgd->rsgqd", probs_n, vals_n, preferred_element_type=jnp.float32
    )
    return mixed.astype(jnp.bfloat16).reshape(rows, steps, width)


def pick(rows, cols, source):
    r = lax.broadcasted_iota(jnp.int32, (rows, cols), 0)
    c = lax.broadcasted_iota(jnp.int32, (rows, cols), 1)
    return source(r, c).astype(jnp.bfloat16)


def shards(
    activations,
    cotangent,
    advantage,
    seq_len,
    key_master,
    moment_one,
    moment_two,
    decode_hidden,
    queries,
    cache_keys,
    cache_values,
    cache_len,
    value_weight,
):
    bf16, f32 = jnp.bfloat16, jnp.float32
    tok_rows, quarter_rows = activations.shape
    sequences = seq_len.shape[0]
    padded_rows = OWN * NX * NY * NZ
    group = lax.axis_index(("x", "y", "z"))
    within = jnp.arange(tok_rows, dtype=jnp.int32)
    length = lax.dynamic_index_in_dim(seq_len, group, keepdims=False)
    adv = lax.dynamic_index_in_dim(advantage, group, keepdims=False).astype(f32) / 256.0
    scale = jnp.where(within < length, adv, f32(0.0)) / sequences
    weighted = (cotangent.astype(f32) * scale[:, None]).astype(bf16)
    padded = jnp.pad(activations, ((0, 0), (0, padded_rows - quarter_rows)))
    partial = lax.dot_general(
        padded, weighted, (((0,), (0,)), ((), ())), preferred_element_type=f32
    ).astype(bf16)
    width = partial.shape[1]

    steps = decode_hidden.shape[1]
    by_quarter = jnp.pad(
        decode_hidden.reshape(steps * TP, quarter_rows), ((0, 0), (0, padded_rows - quarter_rows))
    )
    span = OWN * NZ
    spread = pick(
        padded_rows,
        NZ * NX * NY * PAD,
        lambda r, c: (r // span == (c // PAD) % (NX * NY))
        & (r % span // OWN == c // (NX * NY * PAD))
        & (r % OWN == c % PAD),
    )
    placed_h = jnp.dot(by_quarter, spread, preferred_element_type=f32).astype(bf16)
    placed_h = placed_h.reshape(steps, TP, NZ, HD).transpose(2, 0, 1, 3).reshape(NZ, steps, TP * HD)
    placed_h = jnp.pad(placed_h, ((0, 0), (0, PAD - steps), (0, 0)))

    got = lax.all_to_all(partial, "x", 0, 0, tiled=True)
    part_x = jnp.sum(got.reshape(NX, -1, width).astype(f32), axis=0).astype(bf16)
    blocks = NY * NZ
    stretch = pick(
        blocks * PAD, blocks * OWN, lambda r, c: (r // PAD == c // OWN) & (r % PAD == c % OWN)
    )
    part_x = jnp.dot(stretch, part_x, preferred_element_type=f32).astype(bf16)
    got = lax.all_to_all(part_x, "y", 0, 0, tiled=True)
    part_y = jnp.sum(got.reshape(NY, -1, width).astype(f32), axis=0).astype(bf16)
    packed = jnp.concatenate([part_y.reshape(NZ, PAD, width), placed_h], axis=1)
    got = lax.all_to_all(packed.reshape(NZ * 2 * PAD, width), "z", 0, 0, tiled=True)
    got = got.reshape(NZ, 2 * PAD, width)
    gradient = jnp.sum(got[:, :OWN].astype(f32), axis=0).reshape(key_master.shape)
    hidden_z = got[:, PAD : PAD + steps].reshape(NZ * steps, width)

    corr_one = 1.0 - 0.9**10
    corr_two = 1.0 - 0.95**10
    moment_one_new = 0.9 * moment_one + 0.1 * gradient
    moment_two_new = 0.95 * moment_two + 0.05 * gradient * gradient
    master_new = key_master - 0.005 * (moment_one_new / corr_one) / (
        jnp.sqrt(moment_two_new / corr_two) + 1e-08
    )
    relay = jnp.pad(master_new[0].astype(bf16), ((0, PAD - OWN), (0, 0)))

    heads = relay.reshape(PAD, TP, HD).transpose(1, 0, 2)
    send = jnp.broadcast_to(heads[None], (NX * NY, TP, PAD, HD)).reshape(-1, HD)
    got = lax.all_to_all(send, ("x", "y", "h", "c"), 0, 0, tiled=True)
    weight = got.reshape(NX * NY, TP, PAD, HD).transpose(1, 0, 2, 3).reshape(-1, HD)
    keys_z = jnp.dot(hidden_z, weight, preferred_element_type=f32)
    got = lax.all_to_all(keys_z.reshape(NZ, steps, HD), "z", 0, 0, tiled=True)
    new_keys = jnp.sum(got, axis=0).astype(bf16)[None]

    flat_hidden = decode_hidden.reshape(steps, -1)
    new_values = jnp.dot(flat_hidden, value_weight, preferred_element_type=f32).astype(bf16)[None]
    attention = attend(queries, cache_keys, cache_values, cache_len, new_keys, new_values)
    return (master_new, moment_one_new, moment_two_new, new_keys, new_values, attention)


def solution(mesh):
    grid = Mesh(mesh.devices.reshape(NX, NY, NZ, 2, 2), ("x", "y", "z", "h", "c"))
    grp, tp = ("x", "y", "z"), ("h", "c")
    placed = (
        P(grp, tp),
        P(grp, None),
        P(),
        P(),
        P(tp, grp, None),
        P(tp, grp, None),
        P(tp, grp, None),
        P(grp, None, None),
        P(grp, None, tp),
        P(grp, None, tp),
        P(grp, None, tp),
        P(grp),
        P(None, tp),
    )
    return jax.shard_map(
        shards,
        mesh=grid,
        in_specs=placed,
        out_specs=(
            P(tp, grp, None),
            P(tp, grp, None),
            P(tp, grp, None),
            P(grp, None, tp),
            P(grp, None, tp),
            P(grp, None, tp),
        ),
        check_vma=False,
    )
```

time: 1770 us -> 113 us (0.06)
  waiting for transfers between devices: 995 us -> 45.7 us
  blocking collectives: 490 us -> 0 us
  starting transfers between devices: 243 us -> 48 us
    all_gather x1 -> x0, waiting for transfers between devices: 978 us -> none  [shards(): quarter = lax.all_gather(relay, 'grp', axis=1, tiled=True)]
    unnamed x1 -> x0, blocking collectives: 490 us -> none
    all_to_all x1 -> x5, starting transfers between devices: 146 us -> 48 us  [the longest x1 16.5 us: shards(): lax.all_to_all(packed.reshape(NZ * 2 * PAD, width), 'z', 0, 0, tiled=True)]
    unnamed x24 -> x0, starting transfers between devices: 97 us -> none
    all_to_all x1 -> x5, waiting for transfers between devices: 17 us -> 45.7 us  [the longest x1 11.2 us: shards(): got = lax.all_to_all(partial, 'x', 0, 0, tiled=True)]
  transfers between devices with their start and end apart: 26 -> 5, of which waited for: 2 -> 5; matrix products, arithmetic and copies ran while one was open for 0% -> 4% of each run, Pallas kernels for 0% -> 0%
where the time goes in v1:
time: 113 us
  starting transfers between devices  48 us (42%)
  waiting for transfers between devices  45.7 us (40%)
  matrix products  9 us (8%)
  local copies, waits for them, and re-layouts  4.81 us (4%)
  other arithmetic  2.93 us (3%)
  between operations  2.26 us (2%)
    all_to_all x1, starting transfers between devices, shards(): lax.all_to_all(packed.reshape(NZ * 2 * PAD, width), 'z', 0, 0, tiled=True)  16.5 us
    all_to_all x1, starting transfers between devices, shards(): got = lax.all_to_all(send, ('x', 'y', 'h', 'c'), 0, 0, tiled=True)  12.2 us
    all_to_all x1, waiting for transfers between devices, shards(): got = lax.all_to_all(partial, 'x', 0, 0, tiled=True)  11.2 us
    all_to_all x1, waiting for transfers between devices, shards(): got = lax.all_to_all(send, ('x', 'y', 'h', 'c'), 0, 0, tiled=True)  10.9 us
    all_to_all x1, starting transfers between devices, shards(): got = lax.all_to_all(part_x, 'y', 0, 0, tiled=True)  10.8 us
    all_to_all x1, waiting for transfers between devices, shards(): lax.all_to_all(packed.reshape(NZ * 2 * PAD, width), 'z', 0, 0, tiled=True)  10 us
    all_to_all x1, waiting for transfers between devices, shards(): got = lax.all_to_all(keys_z.reshape(NZ, steps, HD), 'z', 0, 0, tiled=True)  9.19 us
    all_to_all x1, starting transfers between devices, shards(): got = lax.all_to_all(partial, 'x', 0, 0, tiled=True)  4.96 us
  transfers between devices with their start and end apart: 5, of which 5 were waited for; matrix products, arithmetic and copies ran while one was open for 4% of the time, Pallas kernels for 0%

profile of v1, /device:TPU:1, one launch (start us, length us, event | category | flops | bytes accessed | tf_op | source)
XLA Modules:
  0.0 112.7 jit_solution(5743181596830337507)
XLA Ops:
  0.7 1.4 %dynamic_slice.8 = s32[1]{0:T(128)} dynamic-slice(s32[192]{0:T(256)} %param.15, s32[]{:T(128)S(6)} %select_n.78), dynamic_slice_sizes={1} | dynamic-slice | bytes 12 | tf_op jit(solution)/shard_map/jit(dynamic_index_in_dim)/dynamic_slice | solution.py:82
  2.7 1.3 %dynamic_slice.7 = s32[1]{0:T(128)} dynamic-slice(s32[192]{0:T(256)} %param.16, s32[]{:T(128)S(6)} %select_n.78), dynamic_slice_sizes={1} | dynamic-slice | bytes 12 | tf_op jit(solution)/shard_map/jit(dynamic_index_in_dim)/dynamic_slice | solution.py:81
  3.9 0.6 fusion.103
  4.6 2.9 %convolution_convert_fusion = bf16[1344,512]{1,0:T(8,128)(2,1)} fusion(bf16[256,1280]{1,0:T(8,128)(2,1)} %param.13, bf16[256,512]{1,0:T(8,128)(2,1)} %param.14, f32[256]{0:T(256)S(1)} %fusion.103), kind=kOutput, calls=%fused_computation.43 | convolution fusion | flops 353402880 | bytes 2294784 | tf_op jit(solution)/shard_map/dot_general | solution.py:86
  7.5 5.0 %all-to-all-start = ((bf16[4,336,512]{2,1,0:T(8,128)(2,1)}), bf16[4,336,512]{2,1,0:T(8,128)(2,1)S(1)}, u32[]{:S(2)}, u32[]{:S(2)}) async-start(bf16[4,336,512]{2,1,0:T(8,128)(2,1)} %bitcast.64), calls=%async_computation | async-start | bytes 2752512 | tf_op jit(solution)/shard_map/all_to_all | solution.py:107
  12.7 11.2 %all-to-all-done = bf16[4,336,512]{2,1,0:T(8,128)(2,1)S(1)} async-done(((bf16[4,336,512]{2,1,0:T(8,128)(2,1)}), bf16[4,336,512]{2,1,0:T(8,128)(2,1)S(1)}, u32[]{:S(2)}, u32[]{:S(2)}) %all-to-all-start) | async-done | bytes 1376288 | tf_op jit(solution)/shard_map/all_to_all | solution.py:107
  23.9 0.4 reduce_sum.62
  24.3 1.5 %convolution_convert_fusion.1 = bf16[384,512]{1,0:T(8,128)(2,1)} fusion(bf16[336,512]{1,0:T(8,128)(2,1)S(1)} %reduce_sum.62, s32[336]{0:T(512)S(1)} %get-tuple-element.31, s32[336]{0:T(512)S(1)} %get-tuple-element.36, s32[384]{0:T(512)S(1)} %get-tuple-element.33, s32[384]{0:T(512)S(1)} %get-tuple-element.34, s32[336]{0:T(512)S(1)} %get-tuple-element.30, ...), kind=kOutput, calls=%fused_computation.47 | convolution fusion | flops 133220352 | bytes 750240 | tf_op jit(solution)/shard_map/dot_general | solution.py:113
  25.8 10.8 %all-to-all-start.1 = ((bf16[4,96,512]{2,1,0:T(8,128)(2,1)}), bf16[4,96,512]{2,1,0:T(8,128)(2,1)S(1)}, u32[]{:S(2)}, u32[]{:S(2)}) async-start(bf16[4,96,512]{2,1,0:T(8,128)(2,1)} %bitcast.3), calls=%async_computation.1 | async-start | bytes 786432 | tf_op jit(solution)/shard_map/all_to_all | solution.py:114
  36.7 3.2 %fusion.35 = bf16[16,1536]{1,0:T(8,128)(2,1)S(1)} fusion(s32[1536]{0:T(1024)S(1)} %get-tuple-element.16, s32[1536]{0:T(1024)S(1)} %get-tuple-element.17, s32[1344]{0:T(1024)S(1)} %get-tuple-element.18, s32[1344]{0:T(1024)S(1)} %get-tuple-element.22, s32[1536]{0:T(1024)S(1)} %get-tuple-element.14, s32[1536]{0:T(1024)S(1)} %get-tuple-element.28, ...), kind=kOutput, calls=%fused_computation.46 | convolution fusion | flops 128016384 | bytes 167872 | tf_op jit(solution)/shard_map/dot_general | solution.py:103
  40.0 4.4 %all-to-all-done.1 = bf16[4,96,512]{2,1,0:T(8,128)(2,1)S(1)} async-done(((bf16[4,96,512]{2,1,0:T(8,128)(2,1)}), bf16[4,96,512]{2,1,0:T(8,128)(2,1)S(1)}, u32[]{:S(2)}, u32[]{:S(2)}) %all-to-all-start.1) | async-done | bytes 393248 | tf_op jit(solution)/shard_map/all_to_all | solution.py:114
  44.5 0.7 fusion.62
  45.2 16.5 %all-to-all-start.2 = ((bf16[12,16,512]{2,1,0:T(8,128)(2,1)}), bf16[12,16,512]{2,1,0:T(8,128)(2,1)S(1)}, u32[]{:S(2)}, u32[]{:S(2)}) async-start(bf16[12,16,512]{2,1,0:T(8,128)(2,1)} %fusion.62), calls=%async_computation.2 | async-start | bytes 393216 | tf_op jit(solution)/shard_map/all_to_all | solution.py:117
  62.4 0.3 fusion.117
  62.7 10.0 %all-to-all-done.2 = bf16[12,16,512]{2,1,0:T(8,128)(2,1)S(1)} async-done(((bf16[12,16,512]{2,1,0:T(8,128)(2,1)}), bf16[12,16,512]{2,1,0:T(8,128)(2,1)S(1)}, u32[]{:S(2)}, u32[]{:S(2)}) %all-to-all-start.2) | async-done | bytes 196640 | tf_op jit(solution)/shard_map/all_to_all | solution.py:117
  72.8 0.7 fusion.115
  73.5 0.7 broadcast_in_dim.55
  74.2 12.2 %all-to-all-start.3 = ((bf16[64,8,128]{2,1,0:T(8,128)(2,1)}), bf16[64,8,128]{2,1,0:T(8,128)(2,1)S(1)}, u32[]{:S(2)}, u32[]{:S(2)}) async-start(bf16[64,8,128]{2,1,0:T(8,128)(2,1)} %bitcast.8), calls=%async_computation.3 | async-start | bytes 262144 | tf_op jit(solution)/shard_map/all_to_all | solution.py:133
  86.7 10.9 %all-to-all-done.3 = bf16[64,8,128]{2,1,0:T(8,128)(2,1)S(1)} async-done(((bf16[64,8,128]{2,1,0:T(8,128)(2,1)}), bf16[64,8,128]{2,1,0:T(8,128)(2,1)S(1)}, u32[]{:S(2)}, u32[]{:S(2)}) %all-to-all-start.3) | async-done | bytes 131104 | tf_op jit(solution)/shard_map/all_to_all | solution.py:133
  97.9 0.6 copy.27
  98.5 3.5 %all-to-all-start.4 = ((f32[12,4,128]{2,1,0:T(4,128)}), f32[12,4,128]{2,1,0:T(4,128)S(1)}, u32[]{:S(2)}, u32[]{:S(2)}) async-start(f32[12,4,128]{2,1,0:T(4,128)} %copy.27), calls=%async_computation.4 | async-start | bytes 49152 | tf_op jit(solution)/shard_map/all_to_all | solution.py:136
  102.0 9.2 %all-to-all-done.4 = f32[12,4,128]{2,1,0:T(4,128)S(1)} async-done(((f32[12,4,128]{2,1,0:T(4,128)}), f32[12,4,128]{2,1,0:T(4,128)S(1)}, u32[]{:S(2)}, u32[]{:S(2)}) %all-to-all-start.4) | async-done | bytes 24608 | tf_op jit(solution)/shard_map/all_to_all | solution.py:136
  111.6 0.3 convolution_bitcast_fusion
  112.1 0.6 reshape.215
  (58 shorter events, 1.6 us)
Async XLA Ops:
  0.6 85.8 %copy-start = (bf16[5120,128]{1,0:T(8,128)(2,1)S(1)}, bf16[5120,128]{1,0:T(8,128)(2,1)}, u32[]{:S(2)}) copy-start(bf16[5120,128]{1,0:T(8,128)(2,1)} %param.25) | copy-start | bytes 3932164
  7.5 5.1 %copy-start.2 = (bf16[1,4,5120]{2,1,0:T(4,128)(2,1)S(1)}, bf16[1,4,5120]{2,1,0:T(4,128)(2,1)}, u32[]{:S(2)}) copy-start(bf16[1,4,5120]{2,1,0:T(4,128)(2,1)} %param.20) | copy-start | bytes 122884
  7.5 16.5 %all-to-all-start = ((bf16[4,336,512]{2,1,0:T(8,128)(2,1)}), bf16[4,336,512]{2,1,0:T(8,128)(2,1)S(1)}, u32[]{:S(2)}, u32[]{:S(2)}) async-start(bf16[4,336,512]{2,1,0:T(8,128)(2,1)} %bitcast.64), calls=%async_computation | async-start | bytes 2752512 | tf_op jit(solution)/shard_map/all_to_all | solution.py:107
  25.8 18.6 %all-to-all-start.1 = ((bf16[4,96,512]{2,1,0:T(8,128)(2,1)}), bf16[4,96,512]{2,1,0:T(8,128)(2,1)S(1)}, u32[]{:S(2)}, u32[]{:S(2)}) async-start(bf16[4,96,512]{2,1,0:T(8,128)(2,1)} %bitcast.3), calls=%async_computation.1 | async-start | bytes 786432 | tf_op jit(solution)/shard_map/all_to_all | solution.py:114
  39.9 21.8 %copy-start.6 = (bf16[1,4,640]{2,1,0:T(4,128)(2,1)S(1)}, bf16[1,4,640]{2,1,0:T(4,128)(2,1)}, u32[]{:S(2)}) copy-start(bf16[1,4,640]{2,1,0:T(4,128)(2,1)} %param.21) | copy-start | bytes 15364
  39.9 22.5 %copy-start.1 = (bf16[1,2048,128]{2,1,0:T(8,128)(2,1)S(1)}, bf16[1,2048,128]{2,1,0:T(8,128)(2,1)}, u32[]{:S(2)}) copy-start(bf16[1,2048,128]{2,1,0:T(8,128)(2,1)} %param.22) | copy-start | bytes 1572868
  39.9 32.9 %copy-start.3 = (f32[1,7,512]{2,0,1:T(1,128)S(1)}, f32[1,7,512]{2,0,1:T(1,128)}, u32[]{:S(2)}) copy-start(f32[1,7,512]{2,0,1:T(1,128)} %param.17) | copy-start | bytes 43012
  39.9 32.9 %copy-start.4 = (f32[1,7,512]{2,0,1:T(1,128)S(1)}, f32[1,7,512]{2,0,1:T(1,128)}, u32[]{:S(2)}) copy-start(f32[1,7,512]{2,0,1:T(1,128)} %param.18) | copy-start | bytes 43012
  39.9 32.9 %copy-start.5 = (f32[1,7,512]{2,0,1:T(1,128)S(1)}, f32[1,7,512]{2,0,1:T(1,128)}, u32[]{:S(2)}) copy-start(f32[1,7,512]{2,0,1:T(1,128)} %param.19) | copy-start | bytes 43012
  45.2 27.6 %all-to-all-start.2 = ((bf16[12,16,512]{2,1,0:T(8,128)(2,1)}), bf16[12,16,512]{2,1,0:T(8,128)(2,1)S(1)}, u32[]{:S(2)}, u32[]{:S(2)}) async-start(bf16[12,16,512]{2,1,0:T(8,128)(2,1)} %fusion.62), calls=%async_computation.2 | async-start | bytes 393216 | tf_op jit(solution)/shard_map/all_to_all | solution.py:117
  74.2 37.4 %copy-start.9 = (bf16[1,2048,128]{2,1,0:T(8,128)(2,1)S(1)}, bf16[1,2048,128]{2,1,0:T(8,128)(2,1)}, u32[]{:S(2)}) copy-start(bf16[1,2048,128]{2,1,0:T(8,128)(2,1)} %param.23) | copy-start | bytes 1572868
  74.2 23.5 %all-to-all-start.3 = ((bf16[64,8,128]{2,1,0:T(8,128)(2,1)}), bf16[64,8,128]{2,1,0:T(8,128)(2,1)S(1)}, u32[]{:S(2)}, u32[]{:S(2)}) async-start(bf16[64,8,128]{2,1,0:T(8,128)(2,1)} %bitcast.8), calls=%async_computation.3 | async-start | bytes 262144 | tf_op jit(solution)/shard_map/all_to_all | solution.py:133
  86.7 26.0 %copy-start.7 = (bf16[4,128]{1,0:T(4,128)(2,1)}, bf16[4,128]{1,0:T(4,128)(2,1)S(1)}, u32[]{:S(2)}) copy-start(bf16[4,128]{1,0:T(4,128)(2,1)S(1)} %convolution_convert_fusion.2) | copy-start | bytes 3076
  98.5 12.7 %all-to-all-start.4 = ((f32[12,4,128]{2,1,0:T(4,128)}), f32[12,4,128]{2,1,0:T(4,128)S(1)}, u32[]{:S(2)}, u32[]{:S(2)}) async-start(f32[12,4,128]{2,1,0:T(4,128)} %copy.27), calls=%async_computation.4 | async-start | bytes 49152 | tf_op jit(solution)/shard_map/all_to_all | solution.py:136
  111.2 1.5 %copy-start.8 = (bf16[4,128]{1,0:T(4,128)(2,1)}, bf16[4,128]{1,0:T(4,128)(2,1)S(1)}, u32[]{:S(2)}) copy-start(bf16[4,128]{1,0:T(4,128)(2,1)S(1)} %reduce_sum.66) | copy-start | bytes 3076

commit v2 on v1

--- a/solution.py
+++ b/solution.py
@@ -78,8 +78,9 @@
     padded_rows = OWN * NX * NY * NZ
     group = lax.axis_index(("x", "y", "z"))
     within = jnp.arange(tok_rows, dtype=jnp.int32)
-    length = lax.dynamic_index_in_dim(seq_len, group, keepdims=False)
-    adv = lax.dynamic_index_in_dim(advantage, group, keepdims=False).astype(f32) / 256.0
+    mine = jnp.arange(sequences, dtype=jnp.int32) == group
+    length = jnp.sum(jnp.where(mine, seq_len, 0))
+    adv = jnp.sum(jnp.where(mine, advantage, 0)).astype(f32) / 256.0
     scale = jnp.where(within < length, adv, f32(0.0)) / sequences
     weighted = (cotangent.astype(f32) * scale[:, None]).astype(bf16)
     padded = jnp.pad(activations, ((0, 0), (0, padded_rows - quarter_rows)))
@@ -92,32 +93,35 @@
     by_quarter = jnp.pad(
         decode_hidden.reshape(steps * TP, quarter_rows), ((0, 0), (0, padded_rows - quarter_rows))
     )
-    span = OWN * NZ
+    blocks = NY * NZ
+    lanes = NX * PAD
     spread = pick(
         padded_rows,
-        NZ * NX * NY * PAD,
-        lambda r, c: (r // span == (c // PAD) % (NX * NY))
-        & (r % span // OWN == c // (NX * NY * PAD))
+        blocks * lanes,
+        lambda r, c: (r // (OWN * blocks) == c % lanes // PAD)
+        & (r // OWN % blocks == c // lanes)
         & (r % OWN == c % PAD),
     )
     placed_h = jnp.dot(by_quarter, spread, preferred_element_type=f32).astype(bf16)
-    placed_h = placed_h.reshape(steps, TP, NZ, HD).transpose(2, 0, 1, 3).reshape(NZ, steps, TP * HD)
-    placed_h = jnp.pad(placed_h, ((0, 0), (0, PAD - steps), (0, 0)))
+    placed_h = placed_h.reshape(steps * TP, blocks, lanes).transpose(1, 0, 2).reshape(blocks, width)
 
     got = lax.all_to_all(partial, "x", 0, 0, tiled=True)
     part_x = jnp.sum(got.reshape(NX, -1, width).astype(f32), axis=0).astype(bf16)
-    blocks = NY * NZ
     stretch = pick(
-        blocks * PAD, blocks * OWN, lambda r, c: (r // PAD == c // OWN) & (r % PAD == c % OWN)
+        blocks * PAD,
+        blocks * PAD,
+        lambda r, c: jnp.where(
+            c < blocks * OWN,
+            (r // PAD == c // OWN) & (r % PAD == c % OWN),
+            (r // PAD == c - blocks * OWN) & (r % PAD == OWN),
+        ),
     )
-    part_x = jnp.dot(stretch, part_x, preferred_element_type=f32).astype(bf16)
-    got = lax.all_to_all(part_x, "y", 0, 0, tiled=True)
-    part_y = jnp.sum(got.reshape(NY, -1, width).astype(f32), axis=0).astype(bf16)
-    packed = jnp.concatenate([part_y.reshape(NZ, PAD, width), placed_h], axis=1)
-    got = lax.all_to_all(packed.reshape(NZ * 2 * PAD, width), "z", 0, 0, tiled=True)
-    got = got.reshape(NZ, 2 * PAD, width)
+    part_x = jnp.dot(
+        stretch, jnp.concatenate([part_x, placed_h], axis=0), preferred_element_type=f32
+    ).astype(bf16)
+    got = lax.all_to_all(part_x, ("y", "z"), 0, 0, tiled=True).reshape(blocks, PAD, width)
     gradient = jnp.sum(got[:, :OWN].astype(f32), axis=0).reshape(key_master.shape)
-    hidden_z = got[:, PAD : PAD + steps].reshape(NZ * steps, width)
+    hidden_yz = got[:, OWN].reshape(blocks * steps, TP * lanes)
 
     corr_one = 1.0 - 0.9**10
     corr_two = 1.0 - 0.95**10
@@ -129,11 +133,10 @@
     relay = jnp.pad(master_new[0].astype(bf16), ((0, PAD - OWN), (0, 0)))
 
     heads = relay.reshape(PAD, TP, HD).transpose(1, 0, 2)
-    send = jnp.broadcast_to(heads[None], (NX * NY, TP, PAD, HD)).reshape(-1, HD)
-    got = lax.all_to_all(send, ("x", "y", "h", "c"), 0, 0, tiled=True)
-    weight = got.reshape(NX * NY, TP, PAD, HD).transpose(1, 0, 2, 3).reshape(-1, HD)
-    keys_z = jnp.dot(hidden_z, weight, preferred_element_type=f32)
-    got = lax.all_to_all(keys_z.reshape(NZ, steps, HD), "z", 0, 0, tiled=True)
+    send = jnp.broadcast_to(heads[:, None], (TP, NX, PAD, HD)).reshape(-1, HD)
+    weight = lax.all_to_all(send, ("h", "c", "x"), 0, 0, tiled=True)
+    keys_yz = jnp.dot(hidden_yz, weight, preferred_element_type=f32)
+    got = lax.all_to_all(keys_yz.reshape(blocks, steps, HD), ("y", "z"), 0, 0, tiled=True)
     new_keys = jnp.sum(got, axis=0).astype(bf16)[None]
 
     flat_hidden = decode_hidden.reshape(steps, -1)

time: 113 us -> 108 us (0.956)
  starting transfers between devices: 48 us -> 45.8 us
  local copies, waits for them, and re-layouts: 4.81 us -> 2.74 us
  waiting for transfers between devices: 45.7 us -> 44.4 us
    all_to_all x1, waiting for transfers between devices: 11.2 us -> 7.73 us  [shards(): got = lax.all_to_all(partial, 'x', 0, 0, tiled=True)]
    dynamic_slice x2 -> x0, local copies, waits for them, and re-layouts: 2.63 us -> none  [the longest x1 1.36 us: shards(): lax.dynamic_index_in_dim(advantage, group, keepdims=False).astype(f32)]
    all_to_all x4 -> x3, starting transfers between devices: 43 us -> 40.9 us  [the longest x1 25 us: shards(): lax.all_to_all(part_x, ('y', 'z'), 0, 0, tiled=True)]
    all_to_all x4 -> x3, waiting for transfers between devices: 34.5 us -> 36.7 us  [the longest x1 15.3 us: shards(): lax.all_to_all(part_x, ('y', 'z'), 0, 0, tiled=True)]
    reduce_sum x1, other arithmetic: 0.06 us -> 1.44 us  [shards(): adv = jnp.sum(jnp.where(mine, advantage, 0)).astype(f32) / 256.0]
  transfers between devices with their start and end apart: 5 -> 4, of which waited for: 5 -> 4; matrix products, arithmetic and copies ran while one was open for 4% -> 4% of each run, Pallas kernels for 0% -> 0%
where the time goes in v2:
time: 108 us
  starting transfers between devices  45.8 us (42%)
  waiting for transfers between devices  44.4 us (41%)
  matrix products  8.67 us (8%)
  other arithmetic  3.73 us (3%)
  local copies, waits for them, and re-layouts  2.74 us (3%)
  between operations  2.23 us (2%)
    all_to_all x1, starting transfers between devices, shards(): lax.all_to_all(part_x, ('y', 'z'), 0, 0, tiled=True)  25 us
    all_to_all x1, waiting for transfers between devices, shards(): lax.all_to_all(part_x, ('y', 'z'), 0, 0, tiled=True)  15.3 us
    all_to_all x1, waiting for transfers between devices, shards(): lax.all_to_all(keys_yz.reshape(blocks, steps, HD), ('y', 'z'), 0, 0, tile...  11.9 us
    all_to_all x1, starting transfers between devices, shards(): weight = lax.all_to_all(send, ('h', 'c', 'x'), 0, 0, tiled=True)  11.4 us
    all_to_all x1, waiting for transfers between devices, shards(): weight = lax.all_to_all(send, ('h', 'c', 'x'), 0, 0, tiled=True)  9.42 us
    all_to_all x1, waiting for transfers between devices, shards(): got = lax.all_to_all(partial, 'x', 0, 0, tiled=True)  7.73 us
    all_to_all x1, starting transfers between devices, shards(): got = lax.all_to_all(partial, 'x', 0, 0, tiled=True)  4.97 us
    all_to_all x1, starting transfers between devices, shards(): lax.all_to_all(keys_yz.reshape(blocks, steps, HD), ('y', 'z'), 0, 0, tile...  4.52 us
  transfers between devices with their start and end apart: 4, of which 4 were waited for; matrix products, arithmetic and copies ran while one was open for 4% of the time, Pallas kernels for 0%

profile of v2, /device:TPU:1, one launch (start us, length us, event | category | flops | bytes accessed | tf_op | source)
XLA Modules:
  0.0 107.6 jit_solution(1063899752718414939)
XLA Ops:
  0.7 1.4 %select_reduce_fusion = (s32[]{:T(128)}, s32[]{:T(128)}) fusion(s32[192]{0:T(256)} %param.15, s32[]{:T(128)S(6)} %add.88, s32[192]{0:T(256)} %param.16), kind=kLoop, calls=%fused_computation.169 | loop fusion | flops 958 | bytes 1548 | tf_op jit(solution)/shard_map/reduce_sum | solution.py:83
  2.8 0.7 fusion.116
  3.4 2.9 %convolution_convert_fusion = bf16[1344,512]{1,0:T(8,128)(2,1)} fusion(bf16[256,1280]{1,0:T(8,128)(2,1)} %param.13, bf16[256,512]{1,0:T(8,128)(2,1)} %param.14, f32[256]{0:T(256)S(1)} %fusion.116), kind=kOutput, calls=%fused_computation.47 | convolution fusion | flops 353402880 | bytes 2294784 | tf_op jit(solution)/shard_map/dot_general | solution.py:87
  6.3 5.0 %all-to-all-start = ((bf16[4,336,512]{2,1,0:T(8,128)(2,1)}), bf16[4,336,512]{2,1,0:T(8,128)(2,1)S(1)}, u32[]{:S(2)}, u32[]{:S(2)}) async-start(bf16[4,336,512]{2,1,0:T(8,128)(2,1)} %bitcast.66), calls=%async_computation | async-start | bytes 2752512 | tf_op jit(solution)/shard_map/all_to_all | solution.py:108
  11.4 3.0 %fusion.39 = bf16[16,1536]{1,0:T(8,128)(2,1)S(1)} fusion(s32[1536]{0:T(1024)S(1)} %get-tuple-element.18, s32[1536]{0:T(1024)S(1)} %get-tuple-element.22, s32[1344]{0:T(1024)S(1)} %get-tuple-element.15, s32[1344]{0:T(1024)S(1)} %get-tuple-element.17, s32[1536]{0:T(1024)S(1)} %get-tuple-element.19, s32[1536]{0:T(1024)S(1)} %get-tuple-element.23, ...), kind=kOutput, calls=%fused_computation.50 | convolution fusion | flops 132145152 | bytes 167872 | tf_op jit(solution)/shard_map/dot_general | solution.py:105
  15.0 7.7 %all-to-all-done = bf16[4,336,512]{2,1,0:T(8,128)(2,1)S(1)} async-done(((bf16[4,336,512]{2,1,0:T(8,128)(2,1)}), bf16[4,336,512]{2,1,0:T(8,128)(2,1)S(1)}, u32[]{:S(2)}, u32[]{:S(2)}) %all-to-all-start) | async-done | bytes 1376288 | tf_op jit(solution)/shard_map/all_to_all | solution.py:108
  22.8 0.4 reduce_sum.70
  23.1 1.4 %fusion.42 = bf16[48,8,512]{2,1,0:T(8,128)(2,1)} fusion(bf16[48,512]{1,0:T(8,128)(2,1)S(1)} %reshape.186, bf16[336,512]{1,0:T(8,128)(2,1)S(1)} %reduce_sum.70, s32[384]{0:T(512)S(1)} %get-tuple-element.32, s32[384]{0:T(512)S(1)} %get-tuple-element.34, s32[384]{0:T(512)S(1)} %get-tuple-element.40, s32[384]{0:T(512)S(1)} %get-tuple-element.38, ...), kind=kOutput, calls=%fused_computation.52 | convolution fusion | flops 153600000 | bytes 802176 | tf_op jit(solution)/shard_map/dot_general | solution.py:119
  24.5 25.0 %all-to-all-start.1 = ((bf16[48,8,512]{2,1,0:T(8,128)(2,1)}), bf16[48,8,512]{2,1,0:T(8,128)(2,1)S(1)}, u32[]{:S(2)}, u32[]{:S(2)}) async-start(bf16[48,8,512]{2,1,0:T(8,128)(2,1)} %fusion.42), calls=%async_computation.1 | async-start | bytes 786432 | tf_op jit(solution)/shard_map/all_to_all | solution.py:122
  50.2 0.3 fusion.132
  50.5 15.3 %all-to-all-done.1 = bf16[48,8,512]{2,1,0:T(8,128)(2,1)S(1)} async-done(((bf16[48,8,512]{2,1,0:T(8,128)(2,1)}), bf16[48,8,512]{2,1,0:T(8,128)(2,1)S(1)}, u32[]{:S(2)}, u32[]{:S(2)}) %all-to-all-start.1) | async-done | bytes 393248 | tf_op jit(solution)/shard_map/all_to_all | solution.py:122
  66.0 0.7 fusion.130
  66.7 0.6 broadcast_in_dim.61
  67.3 11.4 %all-to-all-start.2 = ((bf16[16,8,128]{2,1,0:T(8,128)(2,1)}), bf16[16,8,128]{2,1,0:T(8,128)(2,1)S(1)}, u32[]{:S(2)}, u32[]{:S(2)}) async-start(bf16[16,8,128]{2,1,0:T(8,128)(2,1)} %bitcast.5), calls=%async_computation.2 | async-start | bytes 65536 | tf_op jit(solution)/shard_map/all_to_all | solution.py:137
  78.7 0.3 slice_reduce_fusion
  79.0 9.4 %all-to-all-done.2 = bf16[16,8,128]{2,1,0:T(8,128)(2,1)S(1)} async-done(((bf16[16,8,128]{2,1,0:T(8,128)(2,1)}), bf16[16,8,128]{2,1,0:T(8,128)(2,1)S(1)}, u32[]{:S(2)}, u32[]{:S(2)}) %all-to-all-start.2) | async-done | bytes 32800 | tf_op jit(solution)/shard_map/all_to_all | solution.py:137
  88.5 0.7 copy.24
  89.2 4.5 %all-to-all-start.3 = ((f32[48,4,128]{2,1,0:T(4,128)}), f32[48,4,128]{2,1,0:T(4,128)S(1)}, u32[]{:S(2)}, u32[]{:S(2)}) async-start(f32[48,4,128]{2,1,0:T(4,128)} %copy.24), calls=%async_computation.3 | async-start | bytes 196608 | tf_op jit(solution)/shard_map/all_to_all | solution.py:139
  93.8 0.3 convolution_convert_fusion.2
  94.0 11.9 %all-to-all-done.3 = f32[48,4,128]{2,1,0:T(4,128)S(1)} async-done(((f32[48,4,128]{2,1,0:T(4,128)}), f32[48,4,128]{2,1,0:T(4,128)S(1)}, u32[]{:S(2)}, u32[]{:S(2)}) %all-to-all-start.3) | async-done | bytes 98336 | tf_op jit(solution)/shard_map/all_to_all | solution.py:139
  106.3 0.2 fusion.74
  106.5 0.3 convolution_bitcast_fusion
  106.8 0.2 fusion.44
  107.0 0.6 reshape.192
  (54 shorter events, 1.2 us)
Async XLA Ops:
  0.6 93.1 %copy-start = (bf16[5120,128]{1,0:T(8,128)(2,1)S(1)}, bf16[5120,128]{1,0:T(8,128)(2,1)}, u32[]{:S(2)}) copy-start(bf16[5120,128]{1,0:T(8,128)(2,1)} %param.25) | copy-start | bytes 3932164
  6.3 5.1 %copy-start.2 = (bf16[1,4,5120]{2,1,0:T(4,128)(2,1)S(1)}, bf16[1,4,5120]{2,1,0:T(4,128)(2,1)}, u32[]{:S(2)}) copy-start(bf16[1,4,5120]{2,1,0:T(4,128)(2,1)} %param.20) | copy-start | bytes 122884
  6.3 16.5 %all-to-all-start = ((bf16[4,336,512]{2,1,0:T(8,128)(2,1)}), bf16[4,336,512]{2,1,0:T(8,128)(2,1)S(1)}, u32[]{:S(2)}, u32[]{:S(2)}) async-start(bf16[4,336,512]{2,1,0:T(8,128)(2,1)} %bitcast.66), calls=%async_computation | async-start | bytes 2752512 | tf_op jit(solution)/shard_map/all_to_all | solution.py:108
  23.1 26.4 %copy-start.6 = (bf16[1,4,640]{2,1,0:T(4,128)(2,1)S(1)}, bf16[1,4,640]{2,1,0:T(4,128)(2,1)}, u32[]{:S(2)}) copy-start(bf16[1,4,640]{2,1,0:T(4,128)(2,1)} %param.21) | copy-start | bytes 15364
  23.1 27.0 %copy-start.1 = (bf16[1,2048,128]{2,1,0:T(8,128)(2,1)S(1)}, bf16[1,2048,128]{2,1,0:T(8,128)(2,1)}, u32[]{:S(2)}) copy-start(bf16[1,2048,128]{2,1,0:T(8,128)(2,1)} %param.22) | copy-start | bytes 1572868
  24.5 41.4 %copy-start.3 = (f32[1,7,512]{2,0,1:T(1,128)S(1)}, f32[1,7,512]{2,0,1:T(1,128)}, u32[]{:S(2)}) copy-start(f32[1,7,512]{2,0,1:T(1,128)} %param.17) | copy-start | bytes 43012
  24.5 41.4 %copy-start.4 = (f32[1,7,512]{2,0,1:T(1,128)S(1)}, f32[1,7,512]{2,0,1:T(1,128)}, u32[]{:S(2)}) copy-start(f32[1,7,512]{2,0,1:T(1,128)} %param.18) | copy-start | bytes 43012
  24.5 41.4 %copy-start.5 = (f32[1,7,512]{2,0,1:T(1,128)S(1)}, f32[1,7,512]{2,0,1:T(1,128)}, u32[]{:S(2)}) copy-start(f32[1,7,512]{2,0,1:T(1,128)} %param.19) | copy-start | bytes 43012
  24.5 41.3 %all-to-all-start.1 = ((bf16[48,8,512]{2,1,0:T(8,128)(2,1)}), bf16[48,8,512]{2,1,0:T(8,128)(2,1)S(1)}, u32[]{:S(2)}, u32[]{:S(2)}) async-start(bf16[48,8,512]{2,1,0:T(8,128)(2,1)} %fusion.42), calls=%async_computation.1 | async-start | bytes 786432 | tf_op jit(solution)/shard_map/all_to_all | solution.py:122
  66.0 40.5 %copy-start.9 = (bf16[1,2048,128]{2,1,0:T(8,128)(2,1)S(1)}, bf16[1,2048,128]{2,1,0:T(8,128)(2,1)}, u32[]{:S(2)}) copy-start(bf16[1,2048,128]{2,1,0:T(8,128)(2,1)} %param.23) | copy-start | bytes 1572868
  67.3 21.1 %all-to-all-start.2 = ((bf16[16,8,128]{2,1,0:T(8,128)(2,1)}), bf16[16,8,128]{2,1,0:T(8,128)(2,1)S(1)}, u32[]{:S(2)}, u32[]{:S(2)}) async-start(bf16[16,8,128]{2,1,0:T(8,128)(2,1)} %bitcast.5), calls=%async_computation.2 | async-start | bytes 65536 | tf_op jit(solution)/shard_map/all_to_all | solution.py:137
  89.2 16.8 %all-to-all-start.3 = ((f32[48,4,128]{2,1,0:T(4,128)}), f32[48,4,128]{2,1,0:T(4,128)S(1)}, u32[]{:S(2)}, u32[]{:S(2)}) async-start(f32[48,4,128]{2,1,0:T(4,128)} %copy.24), calls=%async_computation.3 | async-start | bytes 196608 | tf_op jit(solution)/shard_map/all_to_all | solution.py:139
  94.0 13.5 %copy-start.7 = (bf16[4,128]{1,0:T(4,128)(2,1)}, bf16[4,128]{1,0:T(4,128)(2,1)S(1)}, u32[]{:S(2)}) copy-start(bf16[4,128]{1,0:T(4,128)(2,1)S(1)} %convolution_convert_fusion.2) | copy-start | bytes 3076
  106.1 1.5 %copy-start.8 = (bf16[4,128]{1,0:T(4,128)(2,1)}, bf16[4,128]{1,0:T(4,128)(2,1)S(1)}, u32[]{:S(2)}) copy-start(bf16[4,128]{1,0:T(4,128)(2,1)S(1)} %reduce_sum.73) | copy-start | bytes 3076

commit v3 on v2

v3 whole, which is shorter than its diff:
```python
import math

import jax
import jax.numpy as jnp
import numpy as np
from jax import lax
from jax.experimental import pallas as pl
from jax.experimental.pallas import tpu as pltpu
from jax.sharding import Mesh, PartitionSpec as P

HD = 128
GQA = 5
SEQ = 256
NX, NY, NZ = 4, 4, 12
OWN = 7
PAD = 8
TP = 4


def cache_scores(queries, cache_keys, cache_len):
    rows, steps, width = queries.shape
    length = cache_keys.shape[1]
    heads_kv = cache_keys.shape[2] // HD
    shaped_q = queries.reshape(rows, steps, heads_kv, GQA, HD)
    keys_c = cache_keys.reshape(rows, length, heads_kv, HD)
    score_c = jnp.einsum(
        "rsgqd,rcgd->rgsqc", shaped_q, keys_c, preferred_element_type=jnp.float32
    ) * (1.0 / math.sqrt(HD))
    valid = jnp.arange(length, dtype=jnp.int32)[None, :] < cache_len[:, None]
    score_c = jnp.where(valid[:, None, None, None, :], score_c, -jnp.inf)
    return shaped_q, score_c, jnp.max(score_c, axis=-1)


def attend(shaped_q, score_c, top_c, causal, cache_values, new_keys, new_values):
    rows, steps, heads_kv = shaped_q.shape[:3]
    length = cache_values.shape[1]
    inverse = 1.0 / math.sqrt(HD)
    vals_c = cache_values.reshape(rows, length, heads_kv, HD)
    keys_n = new_keys.reshape(rows, steps, heads_kv, HD)
    vals_n = new_values.reshape(rows, steps, heads_kv, HD)
    score_n = (
        jnp.einsum("rsgqd,rtgd->rgsqt", shaped_q, keys_n, preferred_element_type=jnp.float32)
        * inverse
    )
    score_n = jnp.where(causal[None, None, :, None, :], score_n, -jnp.inf)
    top = jnp.maximum(top_c, jnp.max(score_n, axis=-1))
    exp_c = jnp.exp(score_c - top[..., None])
    exp_n = jnp.exp(score_n - top[..., None])
    total = jnp.sum(exp_c, axis=-1) + jnp.sum(exp_n, axis=-1)
    probs_c = (exp_c / total[..., None]).astype(jnp.bfloat16)
    probs_n = (exp_n / total[..., None]).astype(jnp.bfloat16)
    mixed = jnp.einsum("rgsqc,rcgd->rsgqd", probs_c, vals_c, preferred_element_type=jnp.float32)
    mixed = mixed + jnp.einsum(
        "rgsqt,rtgd->rsgqd", probs_n, vals_n, preferred_element_type=jnp.float32
    )
    return mixed.astype(jnp.bfloat16).reshape(rows, steps, -1)


def pick(target, size):
    c = lax.broadcasted_iota(jnp.int32, (len(target), size), 1)
    return (jnp.asarray(target, jnp.int32)[:, None] == c).astype(jnp.bfloat16)


def gradient_kernel(len_ref, adv_ref, act_ref, cot_ref, out_ref, wgt_ref):
    tok_rows, quarter_rows = act_ref.shape
    group = lax.axis_index(("x", "y", "z"))
    length = len_ref[group]
    adv = adv_ref[group].astype(jnp.float32)
    within = lax.broadcasted_iota(jnp.int32, (tok_rows, HD), 0)
    scale = jnp.where(within < length, adv / 256.0, jnp.float32(0.0)) / len_ref.shape[0]
    for c in range(cot_ref.shape[1] // HD):
        cols = pl.ds(c * HD, HD)
        wgt_ref[:, cols] = (cot_ref[:, cols].astype(jnp.float32) * scale).astype(jnp.bfloat16)
    out_ref[:quarter_rows, :] = lax.dot_general(
        act_ref[...],
        wgt_ref[...],
        (((0,), (0,)), ((), ())),
        preferred_element_type=jnp.float32,
    ).astype(jnp.bfloat16)
    rest = out_ref.shape[0] - quarter_rows
    out_ref[quarter_rows:, :] = jnp.zeros((rest, out_ref.shape[1]), jnp.bfloat16)


def shards(
    activations,
    cotangent,
    advantage,
    seq_len,
    key_master,
    moment_one,
    moment_two,
    decode_hidden,
    queries,
    cache_keys,
    cache_values,
    cache_len,
    value_weight,
):
    bf16, f32 = jnp.bfloat16, jnp.float32
    tok_rows, quarter_rows = activations.shape
    padded_rows = OWN * NX * NY * NZ
    width = cotangent.shape[1]
    smem = pl.BlockSpec(memory_space=pltpu.SMEM)
    vmem = pl.BlockSpec(memory_space=pltpu.VMEM)
    partial = pl.pallas_call(
        gradient_kernel,
        out_shape=jax.ShapeDtypeStruct((padded_rows, width), bf16),
        in_specs=[smem, smem, vmem, vmem],
        out_specs=vmem,
        scratch_shapes=[pltpu.VMEM((tok_rows, width), bf16)],
        name="gradient",
    )(seq_len, advantage, activations, cotangent)

    steps = decode_hidden.shape[1]
    cores = TP // 2
    half = cores * quarter_rows
    mine = lax.dynamic_slice_in_dim(decode_hidden[0], lax.axis_index("h") * half, half, axis=1)
    by_quarter = jnp.pad(
        mine.reshape(steps * cores, quarter_rows), ((0, 0), (0, padded_rows - quarter_rows))
    )
    blocks = NY * NZ
    lanes = NX * PAD
    r = np.arange(padded_rows)
    spread = pick(
        r // OWN % blocks * lanes + r // (OWN * blocks) * PAD + r % OWN, blocks * lanes
    )
    placed_h = jnp.dot(by_quarter, spread, preferred_element_type=f32).astype(bf16)
    used = steps * cores * lanes
    placed_h = placed_h.reshape(steps * cores, blocks, lanes).transpose(1, 0, 2)
    placed_h = jnp.pad(placed_h.reshape(blocks, used), ((0, 0), (0, width - used)))

    r, q = np.arange(blocks * OWN), np.arange(blocks)
    stretch = pick(r // OWN * PAD + r % OWN, blocks * PAD)
    lasts = jnp.dot(
        pick(q * PAD + OWN, blocks * PAD).T, placed_h, preferred_element_type=f32
    ).astype(bf16)

    got = lax.all_to_all(partial, "x", 0, 0, tiled=True)
    part_x = jnp.sum(got.reshape(NX, -1, width).astype(f32), axis=0).astype(bf16)
    part_x = (jnp.dot(stretch.T, part_x, preferred_element_type=f32) + lasts).astype(bf16)
    got = lax.all_to_all(part_x, ("y", "z"), 0, 0, tiled=True).reshape(blocks, PAD, width)
    gradient = jnp.sum(got[:, :OWN].astype(f32), axis=0).reshape(key_master.shape)
    hidden_yz = got[:, OWN, :used].reshape(blocks * steps, cores * lanes)

    corr_one = 1.0 - 0.9**10
    corr_two = 1.0 - 0.95**10
    moment_one_new = 0.9 * moment_one + 0.1 * gradient
    moment_two_new = 0.95 * moment_two + 0.05 * gradient * gradient
    master_new = key_master - 0.005 * (moment_one_new / corr_one) / (
        jnp.sqrt(moment_two_new / corr_two) + 1e-08
    )
    relay = jnp.pad(master_new[0].astype(bf16), ((0, PAD - OWN), (0, 0)))

    heads = relay.reshape(PAD, 2, cores, HD).transpose(2, 0, 1, 3).reshape(cores, PAD, 2 * HD)
    send = jnp.broadcast_to(heads[:, None], (cores, NX, PAD, 2 * HD)).reshape(-1, 2 * HD)
    weight = lax.all_to_all(send, ("c", "x"), 0, 0, tiled=True)
    keys = jnp.stack(
        [jnp.dot(hidden_yz, weight[:, h * HD : (h + 1) * HD], preferred_element_type=f32) for h in range(2)]
    )
    got = lax.all_to_all(keys.reshape(-1, steps, HD), ("h", "y", "z"), 0, 0, tiled=True)
    new_keys = jnp.sum(got, axis=0).astype(bf16)[None]

    flat_hidden = decode_hidden.reshape(steps, -1)
    new_values = jnp.dot(flat_hidden, value_weight, preferred_element_type=f32).astype(bf16)[None]
    shaped_q, score_c, top_c = cache_scores(queries, cache_keys, cache_len)
    causal = (
        jnp.arange(steps, dtype=jnp.int32)[None, :] <= jnp.arange(steps, dtype=jnp.int32)[:, None]
    )
    attention = attend(shaped_q, score_c, top_c, causal, cache_values, new_keys, new_values)
    return (master_new, moment_one_new, moment_two_new, new_keys, new_values, attention)


def solution(mesh):
    grid = Mesh(mesh.devices.reshape(NX, NY, NZ, 2, 2), ("x", "y", "z", "h", "c"))
    grp, tp = ("x", "y", "z"), ("h", "c")
    placed = (
        P(grp, tp),
        P(grp, None),
        P(),
        P(),
        P(tp, grp, None),
        P(tp, grp, None),
        P(tp, grp, None),
        P(grp, None, None),
        P(grp, None, tp),
        P(grp, None, tp),
        P(grp, None, tp),
        P(grp),
        P(None, tp),
    )
    return jax.shard_map(
        shards,
        mesh=grid,
        in_specs=placed,
        out_specs=(
            P(tp, grp, None),
            P(tp, grp, None),
            P(tp, grp, None),
            P(grp, None, tp),
            P(grp, None, tp),
            P(grp, None, tp),
        ),
        check_vma=False,
    )
```

time: 108 us -> 107 us (level); the launches traced: 108 us -> 105 us
  matrix products: 8.67 us -> 5.65 us
  Pallas kernels: 0 us -> 2.95 us
  waiting for transfers between devices: 44.4 us -> 42 us
  other arithmetic: 3.73 us -> 2.21 us
  starting transfers between devices: 45.8 us -> 47 us
    all_to_all x2, waiting for transfers between devices: 21.4 us -> 17.1 us  [the longest x1 12.4 us: shards(): lax.all_to_all(keys.reshape(-1, steps, HD), ('h', 'y', 'z'), 0, 0, tiled=...]
    pallas_call x0 -> x1, Pallas kernels: none -> 2.95 us  [shards(): pl.pallas_call(gradient_kernel, out_shape=jax.ShapeDtypeStruct((padded_ro...]
    unnamed x21 -> x29, local copies, waits for them, and re-layouts: 0.05 us -> 1.92 us
    dot_general x1, matrix products: 3.05 us -> 1.53 us  [shards(): jnp.dot(by_quarter, spread, preferred_element_type=f32).astype(bf16)]
    all_to_all x1, waiting for transfers between devices: 7.73 us -> 9.25 us  [shards(): got = lax.all_to_all(partial, 'x', 0, 0, tiled=True)]
    dot_general x4 -> x5, matrix products: 4.71 us -> 3.2 us  [the longest x1 2.24 us: shards(): jnp.dot(stretch.T, part_x, preferred_element_type=f32) + lasts]
    reduce_sum x1 -> x0, other arithmetic: 1.44 us -> none  [shards(): adv = jnp.sum(jnp.where(mine, advantage, 0)).astype(f32) / 256.0]
    all_to_all x2, starting transfers between devices: 15.9 us -> 17 us  [the longest x1 9.61 us: shards(): weight = lax.all_to_all(send, ('c', 'x'), 0, 0, tiled=True)]
  transfers between devices with their start and end apart: 4 -> 4, of which waited for: 4 -> 4; matrix products, arithmetic and copies ran while one was open for 4% -> 5% of each run, Pallas kernels for 0% -> 0%
where the time goes in v3:
time: 107 us; the launch traced here: 105 us
  starting transfers between devices  47 us (44%)
  waiting for transfers between devices  42 us (39%)
  matrix products  5.65 us (5%)
  local copies, waits for them, and re-layouts  3.73 us (3%)
  Pallas kernels  2.95 us (3%)
  other arithmetic  2.21 us (2%)
  between operations  1.49 us (1%)
    all_to_all x1, starting transfers between devices, shards(): lax.all_to_all(part_x, ('y', 'z'), 0, 0, tiled=True)  25 us
    all_to_all x1, waiting for transfers between devices, shards(): lax.all_to_all(part_x, ('y', 'z'), 0, 0, tiled=True)  15.7 us
    all_to_all x1, waiting for transfers between devices, shards(): lax.all_to_all(keys.reshape(-1, steps, HD), ('h', 'y', 'z'), 0, 0, tiled=...  12.4 us
    all_to_all x1, starting transfers between devices, shards(): weight = lax.all_to_all(send, ('c', 'x'), 0, 0, tiled=True)  9.61 us
    all_to_all x1, waiting for transfers between devices, shards(): got = lax.all_to_all(partial, 'x', 0, 0, tiled=True)  9.25 us
    all_to_all x1, starting transfers between devices, shards(): lax.all_to_all(keys.reshape(-1, steps, HD), ('h', 'y', 'z'), 0, 0, tiled=...  7.42 us
    all_to_all x1, starting transfers between devices, shards(): got = lax.all_to_all(partial, 'x', 0, 0, tiled=True)  4.96 us
    all_to_all x1, waiting for transfers between devices, shards(): weight = lax.all_to_all(send, ('c', 'x'), 0, 0, tiled=True)  4.66 us
  transfers between devices with their start and end apart: 4, of which 4 were waited for; matrix products, arithmetic and copies ran while one was open for 5% of the time, Pallas kernels for 0%

profile of v3, /device:TPU:1, one launch (start us, length us, event | category | flops | bytes accessed | tf_op | source)
XLA Modules:
  0.0 105.0 jit_solution(9440114335226879693)
XLA Ops:
  0.6 2.9 %gradient.1 = bf16[1344,512]{1,0:T(8,128)(2,1)} custom-call(s32[192]{0:T(256)} %len_ref.1, s32[192]{0:T(256)} %adv_ref.1, bf16[256,1280]{1,0:T(8,128)(2,1)} %act_ref.1, bf16[256,512]{1,0:T(8,128)(2,1)} %cot_ref.1), custom_call_target="tpu_custom_call" | custom-call | tf_op jit(solution)/shard_map/gradient/pallas_call | solution.py:105
  3.6 5.0 %all-to-all-start = ((bf16[4,336,512]{2,1,0:T(8,128)(2,1)}), bf16[4,336,512]{2,1,0:T(8,128)(2,1)S(1)}, u32[]{:S(2)}, u32[]{:S(2)}) async-start(bf16[4,336,512]{2,1,0:T(8,128)(2,1)} %bitcast.71), calls=%async_computation | async-start | bytes 2752512 | tf_op jit(solution)/shard_map/all_to_all | solution.py:138
  8.6 1.5 %fusion.3 = bf16[8,1536]{1,0:T(8,128)(2,1)S(1)} fusion(s32[1344]{0:T(1024)S(1)} %copy-done.12, bf16[8,1280]{1,0:T(8,128)(2,1)S(1)} %reshape.181), kind=kOutput, calls=%fused_computation.5 | convolution fusion | flops 35106816 | bytes 50432 | tf_op jit(solution)/shard_map/dot_general | solution.py:127
  10.4 0.4 fusion.5
  10.8 9.2 %all-to-all-done = bf16[4,336,512]{2,1,0:T(8,128)(2,1)S(1)} async-done(((bf16[4,336,512]{2,1,0:T(8,128)(2,1)}), bf16[4,336,512]{2,1,0:T(8,128)(2,1)S(1)}, u32[]{:S(2)}, u32[]{:S(2)}) %all-to-all-start) | async-done | bytes 1376288 | tf_op jit(solution)/shard_map/all_to_all | solution.py:138
  20.1 1.0 reduce_sum.50
  21.1 2.2 %fusion.6 = bf16[48,8,512]{2,1,0:T(8,128)(2,1)} fusion(f32[384,512]{1,0:T(8,128)S(1)} %fusion.5, bf16[336,512]{1,0:T(8,128)(2,1)} %reduce_sum.50, s32[336]{0:T(512)S(1)} %copy-done.7), kind=kOutput, calls=%fused_computation.10 | convolution fusion | flops 132642816 | bytes 1525056 | tf_op jit(solution)/shard_map/dot_general | solution.py:140
  23.3 25.0 %all-to-all-start.1 = ((bf16[48,8,512]{2,1,0:T(8,128)(2,1)}), bf16[48,8,512]{2,1,0:T(8,128)(2,1)S(1)}, u32[]{:S(2)}, u32[]{:S(2)}) async-start(bf16[48,8,512]{2,1,0:T(8,128)(2,1)} %fusion.6), calls=%async_computation.1 | async-start | bytes 786432 | tf_op jit(solution)/shard_map/all_to_all | solution.py:141
  49.0 15.7 %all-to-all-done.1 = bf16[48,8,512]{2,1,0:T(8,128)(2,1)S(1)} async-done(((bf16[48,8,512]{2,1,0:T(8,128)(2,1)}), bf16[48,8,512]{2,1,0:T(8,128)(2,1)S(1)}, u32[]{:S(2)}, u32[]{:S(2)}) %all-to-all-start.1) | async-done | bytes 393248 | tf_op jit(solution)/shard_map/all_to_all | solution.py:141
  64.9 0.6 broadcast_in_dim.31
  65.5 9.6 %all-to-all-start.2 = ((bf16[8,8,256]{2,1,0:T(8,128)(2,1)}), bf16[8,8,256]{2,1,0:T(8,128)(2,1)S(1)}, u32[]{:S(2)}, u32[]{:S(2)}) async-start(bf16[8,8,256]{2,1,0:T(8,128)(2,1)} %bitcast.8), calls=%async_computation.2 | async-start | bytes 65536 | tf_op jit(solution)/shard_map/all_to_all | solution.py:156
  75.3 4.7 %all-to-all-done.2 = bf16[8,8,256]{2,1,0:T(8,128)(2,1)S(1)} async-done(((bf16[8,8,256]{2,1,0:T(8,128)(2,1)}), bf16[8,8,256]{2,1,0:T(8,128)(2,1)S(1)}, u32[]{:S(2)}, u32[]{:S(2)}) %all-to-all-start.2) | async-done | bytes 32800 | tf_op jit(solution)/shard_map/all_to_all | solution.py:156
  80.2 0.7 pad_maximum_fusion
  80.9 7.4 %all-to-all-start.3 = ((f32[96,4,128]{2,1,0:T(4,128)}), f32[96,4,128]{2,1,0:T(4,128)S(1)}, u32[]{:S(2)}, u32[]{:S(2)}) async-start(f32[96,4,128]{2,1,0:T(4,128)} %bitcast.12), calls=%async_computation.3 | async-start | bytes 393216 | tf_op jit(solution)/shard_map/all_to_all | solution.py:160
  88.4 0.3 fusion.35
  88.8 0.3 convolution_convert_fusion.1
  89.0 0.6 copy.38
  89.7 0.6 copy.39
  90.3 0.6 copy.40
  90.9 12.4 %all-to-all-done.3 = f32[96,4,128]{2,1,0:T(4,128)S(1)} async-done(((f32[96,4,128]{2,1,0:T(4,128)}), f32[96,4,128]{2,1,0:T(4,128)S(1)}, u32[]{:S(2)}, u32[]{:S(2)}) %all-to-all-start.3) | async-done | bytes 196640 | tf_op jit(solution)/shard_map/all_to_all | solution.py:160
  103.6 0.2 fusion.14
  103.9 0.3 convolution_bitcast_fusion.2
  104.1 0.2 fusion.8
  104.3 0.6 reshape.189
  (47 shorter events, 1.3 us)
Async XLA Ops:
  0.6 88.1 %copy-start = (bf16[5120,128]{1,0:T(8,128)(2,1)S(1)}, bf16[5120,128]{1,0:T(8,128)(2,1)}, u32[]{:S(2)}) copy-start(bf16[5120,128]{1,0:T(8,128)(2,1)} %param.28) | copy-start | bytes 3932164
  3.6 5.0 %copy-start.2 = (bf16[1,4,5120]{2,1,0:T(4,128)(2,1)S(1)}, bf16[1,4,5120]{2,1,0:T(4,128)(2,1)}, u32[]{:S(2)}) copy-start(bf16[1,4,5120]{2,1,0:T(4,128)(2,1)} %param.23) | copy-start | bytes 122884
  3.6 5.0 %copy-start.12 = (s32[1344]{0:T(1024)S(1)}, s32[1344]{0:T(1024)}, u32[]{:S(2)}) copy-start(s32[1344]{0:T(1024)} %constant.45.clone) | copy-start | bytes 16132
  3.6 16.5 %all-to-all-start = ((bf16[4,336,512]{2,1,0:T(8,128)(2,1)}), bf16[4,336,512]{2,1,0:T(8,128)(2,1)S(1)}, u32[]{:S(2)}, u32[]{:S(2)}) async-start(bf16[4,336,512]{2,1,0:T(8,128)(2,1)} %bitcast.71), calls=%async_computation | async-start | bytes 2752512 | tf_op jit(solution)/shard_map/all_to_all | solution.py:138
  8.6 1.9 %copy-start.10 = (s32[48]{0:T(128)S(1)}, s32[48]{0:T(128)}, u32[]{:S(2)}) copy-start(s32[48]{0:T(128)} %constant.47.clone) | copy-start | bytes 580
  10.3 10.8 %copy-start.7 = (s32[336]{0:T(512)S(1)}, s32[336]{0:T(512)}, u32[]{:S(2)}) copy-start(s32[336]{0:T(512)} %constant.46.clone) | copy-start | bytes 4036
  21.1 27.2 %copy-start.6 = (bf16[1,4,640]{2,1,0:T(4,128)(2,1)S(1)}, bf16[1,4,640]{2,1,0:T(4,128)(2,1)}, u32[]{:S(2)}) copy-start(bf16[1,4,640]{2,1,0:T(4,128)(2,1)} %param.24) | copy-start | bytes 15364
  21.1 43.7 %copy-start.3 = (f32[1,7,512]{2,0,1:T(1,128)S(1)}, f32[1,7,512]{2,0,1:T(1,128)}, u32[]{:S(2)}) copy-start(f32[1,7,512]{2,0,1:T(1,128)} %param.20) | copy-start | bytes 43012
  21.1 43.7 %copy-start.4 = (f32[1,7,512]{2,0,1:T(1,128)S(1)}, f32[1,7,512]{2,0,1:T(1,128)}, u32[]{:S(2)}) copy-start(f32[1,7,512]{2,0,1:T(1,128)} %param.21) | copy-start | bytes 43012
  21.1 43.7 %copy-start.5 = (f32[1,7,512]{2,0,1:T(1,128)S(1)}, f32[1,7,512]{2,0,1:T(1,128)}, u32[]{:S(2)}) copy-start(f32[1,7,512]{2,0,1:T(1,128)} %param.22) | copy-start | bytes 43012
  23.3 65.0 %copy-start.1 = (bf16[1,2048,128]{2,1,0:T(8,128)(2,1)S(1)}, bf16[1,2048,128]{2,1,0:T(8,128)(2,1)}, u32[]{:S(2)}) copy-start(bf16[1,2048,128]{2,1,0:T(8,128)(2,1)} %param.25) | copy-start | bytes 1572868
  23.3 41.3 %all-to-all-start.1 = ((bf16[48,8,512]{2,1,0:T(8,128)(2,1)}), bf16[48,8,512]{2,1,0:T(8,128)(2,1)S(1)}, u32[]{:S(2)}, u32[]{:S(2)}) async-start(bf16[48,8,512]{2,1,0:T(8,128)(2,1)} %fusion.6), calls=%async_computation.1 | async-start | bytes 786432 | tf_op jit(solution)/shard_map/all_to_all | solution.py:141
  65.5 14.5 %all-to-all-start.2 = ((bf16[8,8,256]{2,1,0:T(8,128)(2,1)}), bf16[8,8,256]{2,1,0:T(8,128)(2,1)S(1)}, u32[]{:S(2)}, u32[]{:S(2)}) async-start(bf16[8,8,256]{2,1,0:T(8,128)(2,1)} %bitcast.8), calls=%async_computation.2 | async-start | bytes 65536 | tf_op jit(solution)/shard_map/all_to_all | solution.py:156
  80.9 22.4 %all-to-all-start.3 = ((f32[96,4,128]{2,1,0:T(4,128)}), f32[96,4,128]{2,1,0:T(4,128)S(1)}, u32[]{:S(2)}, u32[]{:S(2)}) async-start(f32[96,4,128]{2,1,0:T(4,128)} %bitcast.12), calls=%async_computation.3 | async-start | bytes 393216 | tf_op jit(solution)/shard_map/all_to_all | solution.py:160
  88.4 15.5 %copy-start.11 = (bf16[1,2048,128]{2,1,0:T(8,128)(2,1)S(1)}, bf16[1,2048,128]{2,1,0:T(8,128)(2,1)}, u32[]{:S(2)}) copy-start(bf16[1,2048,128]{2,1,0:T(8,128)(2,1)} %param.26) | copy-start | bytes 1572868
  89.0 15.9 %copy-start.8 = (bf16[4,128]{1,0:T(4,128)(2,1)}, bf16[4,128]{1,0:T(4,128)(2,1)S(1)}, u32[]{:S(2)}) copy-start(bf16[4,128]{1,0:T(4,128)(2,1)S(1)} %convolution_convert_fusion.1) | copy-start | bytes 3076
  103.4 1.5 %copy-start.9 = (bf16[4,128]{1,0:T(4,128)(2,1)}, bf16[4,128]{1,0:T(4,128)(2,1)S(1)}, u32[]{:S(2)}) copy-start(bf16[4,128]{1,0:T(4,128)(2,1)S(1)} %reduce_sum.53) | copy-start | bytes 3076

commit v4 on v3

--- a/solution.py
+++ b/solution.py
@@ -79,6 +79,27 @@
     ).astype(jnp.bfloat16)
     rest = out_ref.shape[0] - quarter_rows
     out_ref[quarter_rows:, :] = jnp.zeros((rest, out_ref.shape[1]), jnp.bfloat16)
+
+
+def blocks_kernel(got_ref, hidden_ref, out_ref):
+    total = got_ref[0].astype(jnp.float32)
+    for i in range(1, NX):
+        total = total + got_ref[i].astype(jnp.float32)
+    rows, own = out_ref.shape[0], got_ref.shape[1]
+    r = lax.broadcasted_iota(jnp.int32, (rows, own), 0)
+    c = lax.broadcasted_iota(jnp.int32, (rows, own), 1)
+    keep = ((r // PAD) * OWN + r % PAD == c) & (r % PAD < OWN)
+    body = jnp.dot(
+        keep.astype(jnp.bfloat16), total.astype(jnp.bfloat16), preferred_element_type=jnp.float32
+    )
+    count = hidden_ref.shape[0]
+    r = lax.broadcasted_iota(jnp.int32, (rows, count), 0)
+    c = lax.broadcasted_iota(jnp.int32, (rows, count), 1)
+    last = r == c * PAD + OWN
+    body = body + jnp.dot(
+        last.astype(jnp.bfloat16), hidden_ref[...], preferred_element_type=jnp.float32
+    )
+    out_ref[...] = body.astype(jnp.bfloat16)
 
 
 def shards(
@@ -102,6 +123,7 @@
     width = cotangent.shape[1]
     smem = pl.BlockSpec(memory_space=pltpu.SMEM)
     vmem = pl.BlockSpec(memory_space=pltpu.VMEM)
+    small = pltpu.CompilerParams(vmem_limit_bytes=16 * 2**20)
     partial = pl.pallas_call(
         gradient_kernel,
         out_shape=jax.ShapeDtypeStruct((padded_rows, width), bf16),
@@ -112,11 +134,8 @@
     )(seq_len, advantage, activations, cotangent)
 
     steps = decode_hidden.shape[1]
-    cores = TP // 2
-    half = cores * quarter_rows
-    mine = lax.dynamic_slice_in_dim(decode_hidden[0], lax.axis_index("h") * half, half, axis=1)
     by_quarter = jnp.pad(
-        mine.reshape(steps * cores, quarter_rows), ((0, 0), (0, padded_rows - quarter_rows))
+        decode_hidden.reshape(steps * TP, quarter_rows), ((0, 0), (0, padded_rows - quarter_rows))
     )
     blocks = NY * NZ
     lanes = NX * PAD
@@ -125,22 +144,20 @@
         r // OWN % blocks * lanes + r // (OWN * blocks) * PAD + r % OWN, blocks * lanes
     )
     placed_h = jnp.dot(by_quarter, spread, preferred_element_type=f32).astype(bf16)
-    used = steps * cores * lanes
-    placed_h = placed_h.reshape(steps * cores, blocks, lanes).transpose(1, 0, 2)
-    placed_h = jnp.pad(placed_h.reshape(blocks, used), ((0, 0), (0, width - used)))
-
-    r, q = np.arange(blocks * OWN), np.arange(blocks)
-    stretch = pick(r // OWN * PAD + r % OWN, blocks * PAD)
-    lasts = jnp.dot(
-        pick(q * PAD + OWN, blocks * PAD).T, placed_h, preferred_element_type=f32
-    ).astype(bf16)
+    placed_h = placed_h.reshape(steps * TP, blocks, lanes).transpose(1, 0, 2).reshape(blocks, width)
 
     got = lax.all_to_all(partial, "x", 0, 0, tiled=True)
-    part_x = jnp.sum(got.reshape(NX, -1, width).astype(f32), axis=0).astype(bf16)
-    part_x = (jnp.dot(stretch.T, part_x, preferred_element_type=f32) + lasts).astype(bf16)
+    part_x = pl.pallas_call(
+        blocks_kernel,
+        out_shape=jax.ShapeDtypeStruct((blocks * PAD, width), bf16),
+        in_specs=[vmem, vmem],
+        out_specs=vmem,
+        compiler_params=small,
+        name="blocks",
+    )(got.reshape(NX, blocks * OWN, width), placed_h)
     got = lax.all_to_all(part_x, ("y", "z"), 0, 0, tiled=True).reshape(blocks, PAD, width)
     gradient = jnp.sum(got[:, :OWN].astype(f32), axis=0).reshape(key_master.shape)
-    hidden_yz = got[:, OWN, :used].reshape(blocks * steps, cores * lanes)
+    hidden_yz = got[:, OWN].reshape(blocks * steps, TP * lanes)
 
     corr_one = 1.0 - 0.9**10
     corr_two = 1.0 - 0.95**10
@@ -151,21 +168,22 @@
     )
     relay = jnp.pad(master_new[0].astype(bf16), ((0, PAD - OWN), (0, 0)))
 
-    heads = relay.reshape(PAD, 2, cores, HD).transpose(2, 0, 1, 3).reshape(cores, PAD, 2 * HD)
-    send = jnp.broadcast_to(heads[:, None], (cores, NX, PAD, 2 * HD)).reshape(-1, 2 * HD)
-    weight = lax.all_to_all(send, ("c", "x"), 0, 0, tiled=True)
-    keys = jnp.stack(
-        [jnp.dot(hidden_yz, weight[:, h * HD : (h + 1) * HD], preferred_element_type=f32) for h in range(2)]
-    )
-    got = lax.all_to_all(keys.reshape(-1, steps, HD), ("h", "y", "z"), 0, 0, tiled=True)
-    new_keys = jnp.sum(got, axis=0).astype(bf16)[None]
-
+    heads = relay.reshape(PAD, TP, HD).transpose(1, 0, 2)
+    send = jnp.broadcast_to(heads[:, None], (TP, NX, PAD, HD)).reshape(-1, HD)
     flat_hidden = decode_hidden.reshape(steps, -1)
     new_values = jnp.dot(flat_hidden, value_weight, preferred_element_type=f32).astype(bf16)[None]
     shaped_q, score_c, top_c = cache_scores(queries, cache_keys, cache_len)
     causal = (
         jnp.arange(steps, dtype=jnp.int32)[None, :] <= jnp.arange(steps, dtype=jnp.int32)[:, None]
     )
+    send, hidden_yz, new_values, score_c, top_c, causal = lax.optimization_barrier(
+        (send, hidden_yz, new_values, score_c, top_c, causal)
+    )
+    weight = lax.all_to_all(send, ("h", "c", "x"), 0, 0, tiled=True)
+    keys_yz = jnp.dot(hidden_yz, weight, preferred_element_type=f32)
+    got = lax.all_to_all(keys_yz.reshape(blocks, steps, HD), ("y", "z"), 0, 0, tiled=True)
+    new_keys = jnp.sum(got, axis=0).astype(bf16)[None]
+
     attention = attend(shaped_q, score_c, top_c, causal, cache_values, new_keys, new_values)
     return (master_new, moment_one_new, moment_two_new, new_keys, new_values, attention)
 

time: 107 us -> 103 us (0.963); the launches traced: 105 us -> 103 us
  blocking collectives: 0 us -> 37.3 us
  waiting for transfers between devices: 42 us -> 24.4 us
  starting transfers between devices: 47 us -> 29.9 us
  matrix products: 5.65 us -> 2.95 us
  local copies, waits for them, and re-layouts: 3.73 us -> 1.53 us
  Pallas kernels: 2.95 us -> 4.19 us
  other arithmetic: 2.21 us -> 1.12 us
    all_to_all x0 -> x2, blocking collectives: none -> 37.3 us  [the longest x1 20.9 us: shards(): weight = lax.all_to_all(send, ('h', 'c', 'x'), 0, 0, tiled=True)]
    all_to_all x2 -> x0, waiting for transfers between devices: 17.1 us -> none  [the longest x1 12.4 us: shards(): lax.all_to_all(keys.reshape(-1, steps, HD), ('h', 'y', 'z'), 0, 0, tiled=...]
    all_to_all x2 -> x0, starting transfers between devices: 17 us -> none  [the longest x1 9.61 us: shards(): weight = lax.all_to_all(send, ('c', 'x'), 0, 0, tiled=True)]
    dot_general x4 -> x1, matrix products: 2.86 us -> 0.13 us  [shards(): keys_yz = jnp.dot(hidden_yz, weight, preferred_element_type=f32)]
    unnamed x29 -> x23, local copies, waits for them, and re-layouts: 1.92 us -> 0.07 us
    pallas_call x0 -> x1, Pallas kernels: none -> 1.25 us  [shards(): pl.pallas_call(blocks_kernel, out_shape=jax.ShapeDtypeStruct((blocks * PA...]
  transfers between devices with their start and end apart: 4 -> 2, of which waited for: 4 -> 2; matrix products, arithmetic and copies ran while one was open for 5% -> 3% of each run, Pallas kernels for 0% -> 0%
where the time goes in v4:
time: 103 us
  blocking collectives  37.3 us (36%)
  starting transfers between devices  29.9 us (29%)
  waiting for transfers between devices  24.4 us (24%)
  Pallas kernels  4.19 us (4%)
  matrix products  2.95 us (3%)
  local copies, waits for them, and re-layouts  1.53 us (1%)
  between operations  1.49 us (1%)
  other arithmetic  1.12 us (1%)
    all_to_all x1, starting transfers between devices, shards(): lax.all_to_all(part_x, ('y', 'z'), 0, 0, tiled=True)  25 us
    all_to_all x1, blocking collectives, shards(): weight = lax.all_to_all(send, ('h', 'c', 'x'), 0, 0, tiled=True)  20.9 us
    all_to_all x1, blocking collectives, shards(): lax.all_to_all(keys_yz.reshape(blocks, steps, HD), ('y', 'z'), 0, 0, tile...  16.4 us
    all_to_all x1, waiting for transfers between devices, shards(): lax.all_to_all(part_x, ('y', 'z'), 0, 0, tiled=True)  14.9 us
    all_to_all x1, waiting for transfers between devices, shards(): got = lax.all_to_all(partial, 'x', 0, 0, tiled=True)  9.46 us
    all_to_all x1, starting transfers between devices, shards(): got = lax.all_to_all(partial, 'x', 0, 0, tiled=True)  4.97 us
    pallas_call x1, Pallas kernels, shards(): pl.pallas_call(gradient_kernel, out_shape=jax.ShapeDtypeStruct((padded_ro...  2.93 us
  transfers between devices with their start and end apart: 2, of which 2 were waited for; matrix products, arithmetic and copies ran while one was open for 3% of the time, Pallas kernels for 0%

profile of v4, /device:TPU:1, one launch (start us, length us, event | category | flops | bytes accessed | tf_op | source)
XLA Modules:
  0.0 102.9 jit_solution(16648658271862468189)
XLA Ops:
  0.6 2.9 %gradient.1 = bf16[1344,512]{1,0:T(8,128)(2,1)} custom-call(s32[192]{0:T(256)} %len_ref.1, s32[192]{0:T(256)} %adv_ref.1, bf16[256,1280]{1,0:T(8,128)(2,1)} %act_ref.1, bf16[256,512]{1,0:T(8,128)(2,1)} %cot_ref.1), custom_call_target="tpu_custom_call" | custom-call | tf_op jit(solution)/shard_map/gradient/pallas_call | solution.py:127
  3.6 5.0 %all-to-all-start = ((bf16[4,336,512]{2,1,0:T(8,128)(2,1)}), bf16[4,336,512]{2,1,0:T(8,128)(2,1)S(1)}, u32[]{:S(2)}, u32[]{:S(2)}) async-start(bf16[4,336,512]{2,1,0:T(8,128)(2,1)} %bitcast.73), calls=%async_computation | async-start | bytes 2752512 | tf_op jit(solution)/shard_map/all_to_all | solution.py:149
  8.6 1.6 %fusion.3 = bf16[16,1536]{1,0:T(8,128)(2,1)S(1)} fusion(s32[1344]{0:T(1024)S(1)} %copy-done.10, bf16[16,1280]{1,0:T(8,128)(2,1)S(1)} %reshape.158), kind=kOutput, calls=%fused_computation.5 | convolution fusion | flops 68149248 | bytes 95488 | tf_op jit(solution)/shard_map/dot_general | solution.py:146
  10.1 0.2 reshape.159
  10.3 0.1 copy.24
  10.4 0.2 reshape.160.hidden_ref
  10.6 9.5 %all-to-all-done.got_ref = bf16[4,336,512]{2,1,0:T(8,128)(2,1)S(1)} async-done(((bf16[4,336,512]{2,1,0:T(8,128)(2,1)}), bf16[4,336,512]{2,1,0:T(8,128)(2,1)S(1)}, u32[]{:S(2)}, u32[]{:S(2)}) %all-to-all-start) | async-done | bytes 1376288 | tf_op jit(solution)/shard_map/all_to_all | solution.py:149
  20.0 1.3 %blocks.1 = bf16[384,512]{1,0:T(8,128)(2,1)} custom-call(bf16[4,336,512]{2,1,0:T(8,128)(2,1)S(1)} %all-to-all-done.got_ref, bf16[48,512]{1,0:T(8,128)(2,1)S(1)} %reshape.160.hidden_ref), custom_call_target="tpu_custom_call" | custom-call | tf_op jit(solution)/shard_map/blocks/pallas_call | solution.py:150
  21.3 25.0 %all-to-all-start.1 = ((bf16[48,8,512]{2,1,0:T(8,128)(2,1)}), bf16[48,8,512]{2,1,0:T(8,128)(2,1)S(1)}, u32[]{:S(2)}, u32[]{:S(2)}) async-start(bf16[48,8,512]{2,1,0:T(8,128)(2,1)} %bitcast.2), calls=%async_computation.1 | async-start | bytes 786432 | tf_op jit(solution)/shard_map/all_to_all | solution.py:158
  47.0 0.3 fusion.8
  47.3 0.3 fusion.30
  47.7 14.9 %all-to-all-done.1 = bf16[48,8,512]{2,1,0:T(8,128)(2,1)S(1)} async-done(((bf16[48,8,512]{2,1,0:T(8,128)(2,1)}), bf16[48,8,512]{2,1,0:T(8,128)(2,1)S(1)}, u32[]{:S(2)}, u32[]{:S(2)}) %all-to-all-start.1) | async-done | bytes 393248 | tf_op jit(solution)/shard_map/all_to_all | solution.py:158
  62.6 0.1 convert_reduce_fusion
  62.7 0.7 fusion.28
  63.5 0.3 slice_reduce_fusion
  63.8 20.9 %all_to_all.35 = bf16[16,8,128]{2,1,0:T(8,128)(2,1)S(1)} all-to-all(bf16[16,8,128]{2,1,0:T(8,128)(2,1)S(1)} %bitcast.78), channel_id=1, replica_groups=mesh['x'=4,'y'=4,'z'=12,'h'=2,'c'=2] {'h','c','x'}, dimensions={0} | all-to-all | bytes 65536 | tf_op jit(solution)/shard_map/all_to_all | solution.py:182
  84.7 0.1 fusion.14
  84.9 16.4 %all_to_all.36 = f32[48,4,128]{2,1,0:T(4,128)S(1)} all-to-all(f32[48,4,128]{2,1,0:T(4,128)S(1)} %copy.26), channel_id=1, replica_groups=mesh['x'=4,'y'=4,'z'=12,'h'=2,'c'=2] {'y','z'}, dimensions={0} | all-to-all | bytes 196608 | tf_op jit(solution)/shard_map/all_to_all | solution.py:184
  101.3 0.1 reduce_sum.40
  101.4 0.2 fusion.31
  101.6 0.2 fusion.11
  101.8 0.3 convolution_bitcast_fusion
  102.1 0.2 fusion.5
  102.3 0.6 reshape.169
  (34 shorter events, 0.3 us)
Async XLA Ops:
  0.6 46.4 %copy-start = (bf16[5120,128]{1,0:T(8,128)(2,1)S(1)}, bf16[5120,128]{1,0:T(8,128)(2,1)}, u32[]{:S(2)}) copy-start(bf16[5120,128]{1,0:T(8,128)(2,1)} %param.26) | copy-start | bytes 3932164
  3.6 5.0 %copy-start.2 = (bf16[1,4,5120]{2,1,0:T(4,128)(2,1)S(1)}, bf16[1,4,5120]{2,1,0:T(4,128)(2,1)}, u32[]{:S(2)}) copy-start(bf16[1,4,5120]{2,1,0:T(4,128)(2,1)} %param.21) | copy-start | bytes 122884
  3.6 5.0 %copy-start.10 = (s32[1344]{0:T(1024)S(1)}, s32[1344]{0:T(1024)}, u32[]{:S(2)}) copy-start(s32[1344]{0:T(1024)} %constant.30.clone) | copy-start | bytes 16132
  3.6 16.5 %all-to-all-start = ((bf16[4,336,512]{2,1,0:T(8,128)(2,1)}), bf16[4,336,512]{2,1,0:T(8,128)(2,1)S(1)}, u32[]{:S(2)}, u32[]{:S(2)}) async-start(bf16[4,336,512]{2,1,0:T(8,128)(2,1)} %bitcast.73), calls=%async_computation | async-start | bytes 2752512 | tf_op jit(solution)/shard_map/all_to_all | solution.py:149
  10.4 35.9 %copy-start.6 = (bf16[1,4,640]{2,1,0:T(4,128)(2,1)S(1)}, bf16[1,4,640]{2,1,0:T(4,128)(2,1)}, u32[]{:S(2)}) copy-start(bf16[1,4,640]{2,1,0:T(4,128)(2,1)} %param.22) | copy-start | bytes 15364
  21.3 26.0 %copy-start.1 = (bf16[1,2048,128]{2,1,0:T(8,128)(2,1)S(1)}, bf16[1,2048,128]{2,1,0:T(8,128)(2,1)}, u32[]{:S(2)}) copy-start(bf16[1,2048,128]{2,1,0:T(8,128)(2,1)} %param.23) | copy-start | bytes 1572868
  21.3 41.3 %all-to-all-start.1 = ((bf16[48,8,512]{2,1,0:T(8,128)(2,1)}), bf16[48,8,512]{2,1,0:T(8,128)(2,1)S(1)}, u32[]{:S(2)}, u32[]{:S(2)}) async-start(bf16[48,8,512]{2,1,0:T(8,128)(2,1)} %bitcast.2), calls=%async_computation.1 | async-start | bytes 786432 | tf_op jit(solution)/shard_map/all_to_all | solution.py:158
  46.3 16.4 %copy-start.3 = (f32[1,7,512]{2,0,1:T(1,128)S(1)}, f32[1,7,512]{2,0,1:T(1,128)}, u32[]{:S(2)}) copy-start(f32[1,7,512]{2,0,1:T(1,128)} %param.18) | copy-start | bytes 43012
  46.3 16.4 %copy-start.4 = (f32[1,7,512]{2,0,1:T(1,128)S(1)}, f32[1,7,512]{2,0,1:T(1,128)}, u32[]{:S(2)}) copy-start(f32[1,7,512]{2,0,1:T(1,128)} %param.19) | copy-start | bytes 43012
  46.3 16.4 %copy-start.5 = (f32[1,7,512]{2,0,1:T(1,128)S(1)}, f32[1,7,512]{2,0,1:T(1,128)}, u32[]{:S(2)}) copy-start(f32[1,7,512]{2,0,1:T(1,128)} %param.20) | copy-start | bytes 43012
  47.3 54.8 %copy-start.7 = (bf16[1,4,128]{2,1,0:T(4,128)(2,1)}, bf16[1,4,128]{2,1,0:T(4,128)(2,1)S(1)}, u32[]{:S(2)}) copy-start(bf16[1,4,128]{2,1,0:T(4,128)(2,1)S(1)} %fusion.8) | copy-start | bytes 3076
  47.3 54.5 %copy-start.9 = (bf16[1,2048,128]{2,1,0:T(8,128)(2,1)S(1)}, bf16[1,2048,128]{2,1,0:T(8,128)(2,1)}, u32[]{:S(2)}) copy-start(bf16[1,2048,128]{2,1,0:T(8,128)(2,1)} %param.24) | copy-start | bytes 1572868
  101.4 1.5 %copy-start.8 = (bf16[4,128]{1,0:T(4,128)(2,1)}, bf16[4,128]{1,0:T(4,128)(2,1)S(1)}, u32[]{:S(2)}) copy-start(bf16[4,128]{1,0:T(4,128)(2,1)S(1)} %reduce_sum.40) | copy-start | bytes 3076

commit v5 on v4

--- a/solution.py
+++ b/solution.py
@@ -88,7 +88,8 @@
     rows, own = out_ref.shape[0], got_ref.shape[1]
     r = lax.broadcasted_iota(jnp.int32, (rows, own), 0)
     c = lax.broadcasted_iota(jnp.int32, (rows, own), 1)
-    keep = ((r // PAD) * OWN + r % PAD == c) & (r % PAD < OWN)
+    block = r // PAD
+    keep = ((block % NY * NZ + block // NY) * OWN + r % PAD == c) & (r % PAD < OWN)
     body = jnp.dot(
         keep.astype(jnp.bfloat16), total.astype(jnp.bfloat16), preferred_element_type=jnp.float32
     )
@@ -140,13 +141,23 @@
     blocks = NY * NZ
     lanes = NX * PAD
     r = np.arange(padded_rows)
+    block = r // OWN % NZ * NY + r // (OWN * NZ) % NY
     spread = pick(
-        r // OWN % blocks * lanes + r // (OWN * blocks) * PAD + r % OWN, blocks * lanes
+        block * lanes + r // (OWN * blocks) * PAD + r % OWN, blocks * lanes
     )
     placed_h = jnp.dot(by_quarter, spread, preferred_element_type=f32).astype(bf16)
     placed_h = placed_h.reshape(steps * TP, blocks, lanes).transpose(1, 0, 2).reshape(blocks, width)
 
     got = lax.all_to_all(partial, "x", 0, 0, tiled=True)
+    flat_hidden = decode_hidden.reshape(steps, -1)
+    new_values = jnp.dot(flat_hidden, value_weight, preferred_element_type=f32).astype(bf16)[None]
+    shaped_q, score_c, top_c = cache_scores(queries, cache_keys, cache_len)
+    causal = (
+        jnp.arange(steps, dtype=jnp.int32)[None, :] <= jnp.arange(steps, dtype=jnp.int32)[:, None]
+    )
+    got, placed_h, new_values, score_c, top_c, causal = lax.optimization_barrier(
+        (got, placed_h, new_values, score_c, top_c, causal)
+    )
     part_x = pl.pallas_call(
         blocks_kernel,
         out_shape=jax.ShapeDtypeStruct((blocks * PAD, width), bf16),
@@ -155,7 +166,7 @@
         compiler_params=small,
         name="blocks",
     )(got.reshape(NX, blocks * OWN, width), placed_h)
-    got = lax.all_to_all(part_x, ("y", "z"), 0, 0, tiled=True).reshape(blocks, PAD, width)
+    got = lax.all_to_all(part_x, ("z", "y"), 0, 0, tiled=True).reshape(blocks, PAD, width)
     gradient = jnp.sum(got[:, :OWN].astype(f32), axis=0).reshape(key_master.shape)
     hidden_yz = got[:, OWN].reshape(blocks * steps, TP * lanes)
 
@@ -170,18 +181,10 @@
 
     heads = relay.reshape(PAD, TP, HD).transpose(1, 0, 2)
     send = jnp.broadcast_to(heads[:, None], (TP, NX, PAD, HD)).reshape(-1, HD)
-    flat_hidden = decode_hidden.reshape(steps, -1)
-    new_values = jnp.dot(flat_hidden, value_weight, preferred_element_type=f32).astype(bf16)[None]
-    shaped_q, score_c, top_c = cache_scores(queries, cache_keys, cache_len)
-    causal = (
-        jnp.arange(steps, dtype=jnp.int32)[None, :] <= jnp.arange(steps, dtype=jnp.int32)[:, None]
-    )
-    send, hidden_yz, new_values, score_c, top_c, causal = lax.optimization_barrier(
-        (send, hidden_yz, new_values, score_c, top_c, causal)
-    )
+    send, hidden_yz = lax.optimization_barrier((send, hidden_yz))
     weight = lax.all_to_all(send, ("h", "c", "x"), 0, 0, tiled=True)
     keys_yz = jnp.dot(hidden_yz, weight, preferred_element_type=f32)
-    got = lax.all_to_all(keys_yz.reshape(blocks, steps, HD), ("y", "z"), 0, 0, tiled=True)
+    got = lax.all_to_all(keys_yz.reshape(blocks, steps, HD), ("z", "y"), 0, 0, tiled=True)
     new_keys = jnp.sum(got, axis=0).astype(bf16)[None]
 
     attention = attend(shaped_q, score_c, top_c, causal, cache_values, new_keys, new_values)

time: 103 us -> 102 us (level)
  blocking collectives: 37.3 us -> 77.8 us
  starting transfers between devices: 29.9 us -> 4.97 us
  waiting for transfers between devices: 24.4 us -> 7.07 us
  matrix products: 2.95 us -> 4 us
    all_to_all x1 -> x2, blocking collectives: 16.4 us -> 60.3 us  [the longest x1 43.9 us: shards(): lax.all_to_all(part_x, ('z', 'y'), 0, 0, tiled=True)]
    all_to_all x1 -> x0, starting transfers between devices: 25 us -> none  [shards(): lax.all_to_all(part_x, ('y', 'z'), 0, 0, tiled=True)]
    all_to_all x1 -> x0, waiting for transfers between devices: 14.9 us -> none  [shards(): lax.all_to_all(part_x, ('y', 'z'), 0, 0, tiled=True)]
    all_to_all x1, blocking collectives: 20.9 us -> 17.6 us  [shards(): weight = lax.all_to_all(send, ('h', 'c', 'x'), 0, 0, tiled=True)]
    all_to_all x1, waiting for transfers between devices: 9.46 us -> 7.07 us  [shards(): got = lax.all_to_all(partial, 'x', 0, 0, tiled=True)]
    dot_general x1, matrix products: 0.34 us -> 1.4 us  [cache_scores(): jnp.einsum('rsgqd,rcgd->rgsqc', shaped_q, keys_c, preferred_element_type=...]
  transfers between devices with their start and end apart: 2 -> 1, of which waited for: 2 -> 1; matrix products, arithmetic and copies ran while one was open for 3% -> 4% of each run, Pallas kernels for 0% -> 0%
where the time goes in v5:
time: 102 us; the launch traced here: 101 us
  blocking collectives  77.8 us (76%)
  waiting for transfers between devices  7.07 us (7%)
  starting transfers between devices  4.97 us (5%)
  matrix products  4 us (4%)
  Pallas kernels  3.51 us (3%)
  local copies, waits for them, and re-layouts  1.52 us (1%)
  between operations  1.47 us (1%)
  other arithmetic  1.12 us (1%)
    all_to_all x1, blocking collectives, shards(): lax.all_to_all(part_x, ('z', 'y'), 0, 0, tiled=True)  43.9 us
    all_to_all x1, blocking collectives, shards(): weight = lax.all_to_all(send, ('h', 'c', 'x'), 0, 0, tiled=True)  17.6 us
    all_to_all x1, blocking collectives, shards(): lax.all_to_all(keys_yz.reshape(blocks, steps, HD), ('z', 'y'), 0, 0, tile...  16.3 us
    all_to_all x1, waiting for transfers between devices, shards(): got = lax.all_to_all(partial, 'x', 0, 0, tiled=True)  7.07 us
    all_to_all x1, starting transfers between devices, shards(): got = lax.all_to_all(partial, 'x', 0, 0, tiled=True)  4.97 us
    pallas_call x1, Pallas kernels, shards(): pl.pallas_call(gradient_kernel, out_shape=jax.ShapeDtypeStruct((padded_ro...  2.93 us
  transfers between devices with their start and end apart: 1, of which 1 were waited for; matrix products, arithmetic and copies ran while one was open for 4% of the time, Pallas kernels for 0%

profile of v5, /device:TPU:1, one launch (start us, length us, event | category | flops | bytes accessed | tf_op | source)
XLA Modules:
  0.0 101.5 jit_solution(3972402953780397331)
XLA Ops:
  0.6 0.0 copy-start
  0.6 2.9 %gradient.1 = bf16[1344,512]{1,0:T(8,128)(2,1)} custom-call(s32[192]{0:T(256)} %len_ref.1, s32[192]{0:T(256)} %adv_ref.1, bf16[256,1280]{1,0:T(8,128)(2,1)} %act_ref.1, bf16[256,512]{1,0:T(8,128)(2,1)} %cot_ref.1), custom_call_target="tpu_custom_call" | custom-call | tf_op jit(solution)/shard_map/gradient/pallas_call | solution.py:128
  3.6 5.0 %all-to-all-start = ((bf16[4,336,512]{2,1,0:T(8,128)(2,1)}), bf16[4,336,512]{2,1,0:T(8,128)(2,1)S(1)}, u32[]{:S(2)}, u32[]{:S(2)}) async-start(bf16[4,336,512]{2,1,0:T(8,128)(2,1)} %bitcast.76), calls=%async_computation | async-start | bytes 2752512 | tf_op jit(solution)/shard_map/all_to_all | solution.py:151
  8.6 1.6 %fusion.3 = bf16[16,1536]{1,0:T(8,128)(2,1)S(1)} fusion(s32[1344]{0:T(1024)S(1)} %copy-done.9, bf16[16,1280]{1,0:T(8,128)(2,1)S(1)} %reshape.159), kind=kOutput, calls=%fused_computation.5 | convolution fusion | flops 68149248 | bytes 95488 | tf_op jit(solution)/shard_map/dot_general | solution.py:148
  10.2 0.2 reshape.160
  10.3 0.1 copy.24
  10.4 0.2 reshape.161.hidden_ref
  11.3 0.3 fusion.8
  11.6 1.4 %fusion.30 = (f32[4,5]{1,0:T(4,128)S(1)}, f32[4,5,2048]{2,1,0:T(8,128)S(1)}) fusion(bf16[4,5,128]{2,1,0:T(8,128)(2,1)S(1)} %reshape.163, bf16[1,2048,128]{2,1,0:T(8,128)(2,1)} %param.23, pred[2048]{0:T(1024)(128)(4,1)S(1)} %iota_compare_fusion.4), kind=kOutput, calls=%fused_computation.50 | convolution fusion | flops 10608620 | bytes 695376 | tf_op jit(solution)/shard_map/rsgqd,rcgd->rgsqc/dot_general | solution.py:26
  13.0 7.1 %all-to-all-done = bf16[4,336,512]{2,1,0:T(8,128)(2,1)S(1)} async-done(((bf16[4,336,512]{2,1,0:T(8,128)(2,1)}), bf16[4,336,512]{2,1,0:T(8,128)(2,1)S(1)}, u32[]{:S(2)}, u32[]{:S(2)}) %all-to-all-start) | async-done | bytes 1376288 | tf_op jit(solution)/shard_map/all_to_all | solution.py:151
  20.1 0.6 blocks.1
  20.7 43.9 %all_to_all.38 = bf16[48,8,512]{2,1,0:T(8,128)(2,1)S(1)} all-to-all(bf16[48,8,512]{2,1,0:T(8,128)(2,1)S(1)} %bitcast.75), channel_id=1, replica_groups=mesh['x'=4,'y'=4,'z'=12,'h'=2,'c'=2] {'z','y'}, dimensions={0} | all-to-all | bytes 786432 | tf_op jit(solution)/shard_map/all_to_all | solution.py:169
  64.6 0.1 convert_reduce_fusion
  64.7 0.7 fusion.28
  65.4 0.3 slice_reduce_fusion
  65.8 17.6 %all_to_all.39 = bf16[16,8,128]{2,1,0:T(8,128)(2,1)S(1)} all-to-all(bf16[16,8,128]{2,1,0:T(8,128)(2,1)S(1)} %bitcast.81), channel_id=1, replica_groups=mesh['x'=4,'y'=4,'z'=12,'h'=2,'c'=2] {'h','c','x'}, dimensions={0} | all-to-all | bytes 65536 | tf_op jit(solution)/shard_map/all_to_all | solution.py:185
  83.4 0.1 fusion.14
  83.5 16.3 %all_to_all.40 = f32[48,4,128]{2,1,0:T(4,128)S(1)} all-to-all(f32[48,4,128]{2,1,0:T(4,128)S(1)} %copy.26), channel_id=1, replica_groups=mesh['x'=4,'y'=4,'z'=12,'h'=2,'c'=2] {'z','y'}, dimensions={0} | all-to-all | bytes 196608 | tf_op jit(solution)/shard_map/all_to_all | solution.py:187
  99.9 0.1 reduce_sum.40
  99.9 0.2 fusion.31
  100.1 0.2 fusion.11
  100.4 0.3 convolution_bitcast_fusion
  100.7 0.2 fusion.5
  100.9 0.6 reshape.171
  (31 shorter events, 0.2 us)
Async XLA Ops:
  0.6 10.7 %copy-start = (bf16[5120,128]{1,0:T(8,128)(2,1)S(1)}, bf16[5120,128]{1,0:T(8,128)(2,1)}, u32[]{:S(2)}) copy-start(bf16[5120,128]{1,0:T(8,128)(2,1)} %param.26) | copy-start | bytes 3932164
  3.6 5.0 %copy-start.1 = (bf16[1,4,5120]{2,1,0:T(4,128)(2,1)S(1)}, bf16[1,4,5120]{2,1,0:T(4,128)(2,1)}, u32[]{:S(2)}) copy-start(bf16[1,4,5120]{2,1,0:T(4,128)(2,1)} %param.21) | copy-start | bytes 122884
  3.6 5.0 %copy-start.9 = (s32[1344]{0:T(1024)S(1)}, s32[1344]{0:T(1024)}, u32[]{:S(2)}) copy-start(s32[1344]{0:T(1024)} %constant.30.clone) | copy-start | bytes 16132
  3.6 16.5 %all-to-all-start = ((bf16[4,336,512]{2,1,0:T(8,128)(2,1)}), bf16[4,336,512]{2,1,0:T(8,128)(2,1)S(1)}, u32[]{:S(2)}, u32[]{:S(2)}) async-start(bf16[4,336,512]{2,1,0:T(8,128)(2,1)} %bitcast.76), calls=%async_computation | async-start | bytes 2752512 | tf_op jit(solution)/shard_map/all_to_all | solution.py:151
  8.6 2.0 %copy-start.5 = (bf16[1,4,640]{2,1,0:T(4,128)(2,1)S(1)}, bf16[1,4,640]{2,1,0:T(4,128)(2,1)}, u32[]{:S(2)}) copy-start(bf16[1,4,640]{2,1,0:T(4,128)(2,1)} %param.22) | copy-start | bytes 15364
  11.6 89.1 %copy-start.6 = (bf16[1,4,128]{2,1,0:T(4,128)(2,1)}, bf16[1,4,128]{2,1,0:T(4,128)(2,1)S(1)}, u32[]{:S(2)}) copy-start(bf16[1,4,128]{2,1,0:T(4,128)(2,1)S(1)} %fusion.8) | copy-start | bytes 3076
  20.0 44.7 %copy-start.2 = (f32[1,7,512]{2,0,1:T(1,128)S(1)}, f32[1,7,512]{2,0,1:T(1,128)}, u32[]{:S(2)}) copy-start(f32[1,7,512]{2,0,1:T(1,128)} %param.18) | copy-start | bytes 43012
  20.1 44.7 %copy-start.3 = (f32[1,7,512]{2,0,1:T(1,128)S(1)}, f32[1,7,512]{2,0,1:T(1,128)}, u32[]{:S(2)}) copy-start(f32[1,7,512]{2,0,1:T(1,128)} %param.19) | copy-start | bytes 43012
  20.1 44.7 %copy-start.4 = (f32[1,7,512]{2,0,1:T(1,128)S(1)}, f32[1,7,512]{2,0,1:T(1,128)}, u32[]{:S(2)}) copy-start(f32[1,7,512]{2,0,1:T(1,128)} %param.20) | copy-start | bytes 43012
  20.6 79.7 %copy-start.8 = (bf16[1,2048,128]{2,1,0:T(8,128)(2,1)S(1)}, bf16[1,2048,128]{2,1,0:T(8,128)(2,1)}, u32[]{:S(2)}) copy-start(bf16[1,2048,128]{2,1,0:T(8,128)(2,1)} %param.24) | copy-start | bytes 1572868
  99.9 1.6 %copy-start.7 = (bf16[4,128]{1,0:T(4,128)(2,1)}, bf16[4,128]{1,0:T(4,128)(2,1)S(1)}, u32[]{:S(2)}) copy-start(bf16[4,128]{1,0:T(4,128)(2,1)S(1)} %reduce_sum.40) | copy-start | bytes 3076

commit v6 on v5

--- a/solution.py
+++ b/solution.py
@@ -15,6 +15,7 @@
 OWN = 7
 PAD = 8
 TP = 4
+CHUNK = 256
 
 
 def cache_scores(queries, cache_keys, cache_len):
@@ -61,24 +62,47 @@
     return (jnp.asarray(target, jnp.int32)[:, None] == c).astype(jnp.bfloat16)
 
 
-def gradient_kernel(len_ref, adv_ref, act_ref, cot_ref, out_ref, wgt_ref):
+def gradient_kernel(
+    len_ref, adv_ref, act_hbm, cot_hbm, out_hbm, act_ref, cot_ref, wgt_ref, out_ref, sem
+):
     tok_rows, quarter_rows = act_ref.shape
+    parts = quarter_rows // CHUNK
+    cot_in = pltpu.make_async_copy(cot_hbm, cot_ref, sem.at[0])
+    cot_in.start()
+    loads, stores = [], []
+    for i in range(parts):
+        cols = pl.ds(i * CHUNK, CHUNK)
+        loads.append(
+            pltpu.make_async_copy(act_hbm.at[:, cols], act_ref.at[:, cols], sem.at[1 + i])
+        )
+        loads[i].start()
+        end = (i + 1) * CHUNK if i + 1 < parts else out_ref.shape[0]
+        rows = pl.ds(i * CHUNK, end - i * CHUNK)
+        stores.append(
+            pltpu.make_async_copy(out_ref.at[rows], out_hbm.at[rows], sem.at[1 + parts + i])
+        )
+    rest = out_ref.shape[0] - quarter_rows
+    out_ref[quarter_rows:, :] = jnp.zeros((rest, out_ref.shape[1]), jnp.bfloat16)
     group = lax.axis_index(("x", "y", "z"))
     length = len_ref[group]
     adv = adv_ref[group].astype(jnp.float32)
     within = lax.broadcasted_iota(jnp.int32, (tok_rows, HD), 0)
     scale = jnp.where(within < length, adv / 256.0, jnp.float32(0.0)) / len_ref.shape[0]
+    cot_in.wait()
     for c in range(cot_ref.shape[1] // HD):
         cols = pl.ds(c * HD, HD)
         wgt_ref[:, cols] = (cot_ref[:, cols].astype(jnp.float32) * scale).astype(jnp.bfloat16)
-    out_ref[:quarter_rows, :] = lax.dot_general(
-        act_ref[...],
-        wgt_ref[...],
-        (((0,), (0,)), ((), ())),
-        preferred_element_type=jnp.float32,
-    ).astype(jnp.bfloat16)
-    rest = out_ref.shape[0] - quarter_rows
-    out_ref[quarter_rows:, :] = jnp.zeros((rest, out_ref.shape[1]), jnp.bfloat16)
+    for i in range(parts):
+        loads[i].wait()
+        out_ref[i * CHUNK : (i + 1) * CHUNK, :] = lax.dot_general(
+            act_ref[:, i * CHUNK : (i + 1) * CHUNK],
+            wgt_ref[...],
+            (((0,), (0,)), ((), ())),
+            preferred_element_type=jnp.float32,
+        ).astype(jnp.bfloat16)
+        stores[i].start()
+    for i in range(parts):
+        stores[i].wait()
 
 
 def blocks_kernel(got_ref, hidden_ref, out_ref):
@@ -124,13 +148,20 @@
     width = cotangent.shape[1]
     smem = pl.BlockSpec(memory_space=pltpu.SMEM)
     vmem = pl.BlockSpec(memory_space=pltpu.VMEM)
+    hbm = pl.BlockSpec(memory_space=pl.ANY)
     small = pltpu.CompilerParams(vmem_limit_bytes=16 * 2**20)
     partial = pl.pallas_call(
         gradient_kernel,
         out_shape=jax.ShapeDtypeStruct((padded_rows, width), bf16),
-        in_specs=[smem, smem, vmem, vmem],
-        out_specs=vmem,
-        scratch_shapes=[pltpu.VMEM((tok_rows, width), bf16)],
+        in_specs=[smem, smem, hbm, hbm],
+        out_specs=hbm,
+        scratch_shapes=[
+            pltpu.VMEM((tok_rows, quarter_rows), bf16),
+            pltpu.VMEM((tok_rows, width), bf16),
+            pltpu.VMEM((tok_rows, width), bf16),
+            pltpu.VMEM((padded_rows, width), bf16),
+            pltpu.SemaphoreType.DMA((1 + 2 * (quarter_rows // CHUNK),)),
+        ],
         name="gradient",
     )(seq_len, advantage, activations, cotangent)
 

time: 102 us -> 103 us (level)
  no operation moved by 1% of the time
where the time goes in v6:
time: 103 us
  blocking collectives  77.8 us (76%)
  waiting for transfers between devices  7.07 us (7%)
  starting transfers between devices  4.98 us (5%)
  Pallas kernels  4.51 us (4%)
  matrix products  4 us (4%)
  local copies, waits for them, and re-layouts  1.53 us (1%)
  between operations  1.49 us (1%)
  other arithmetic  1.12 us (1%)
    all_to_all x1, blocking collectives, shards(): lax.all_to_all(part_x, ('z', 'y'), 0, 0, tiled=True)  43.9 us
    all_to_all x1, blocking collectives, shards(): weight = lax.all_to_all(send, ('h', 'c', 'x'), 0, 0, tiled=True)  17.6 us
    all_to_all x1, blocking collectives, shards(): lax.all_to_all(keys_yz.reshape(blocks, steps, HD), ('z', 'y'), 0, 0, tile...  16.3 us
    all_to_all x1, waiting for transfers between devices, shards(): got = lax.all_to_all(partial, 'x', 0, 0, tiled=True)  7.07 us
    all_to_all x1, starting transfers between devices, shards(): got = lax.all_to_all(partial, 'x', 0, 0, tiled=True)  4.98 us
    pallas_call x1, Pallas kernels, shards(): pl.pallas_call(gradient_kernel, out_shape=jax.ShapeDtypeStruct((padded_ro...  3.93 us
  transfers between devices with their start and end apart: 1, of which 1 were waited for; matrix products, arithmetic and copies ran while one was open for 4% of the time, Pallas kernels for 0%

profile of v6, /device:TPU:1, one launch (start us, length us, event | category | flops | bytes accessed | tf_op | source)
XLA Modules:
  0.0 102.5 jit_solution(317166012556892794)
XLA Ops:
  0.6 0.0 copy-start
  0.6 3.9 %gradient.1 = bf16[1344,512]{1,0:T(8,128)(2,1)} custom-call(s32[192]{0:T(256)} %len_ref.1, s32[192]{0:T(256)} %adv_ref.1, bf16[256,1280]{1,0:T(8,128)(2,1)} %act_hbm.1, bf16[256,512]{1,0:T(8,128)(2,1)} %cot_hbm.1), custom_call_target="tpu_custom_call" | custom-call | tf_op jit(solution)/shard_map/gradient/pallas_call | solution.py:153
  4.6 5.0 %all-to-all-start = ((bf16[4,336,512]{2,1,0:T(8,128)(2,1)}), bf16[4,336,512]{2,1,0:T(8,128)(2,1)S(1)}, u32[]{:S(2)}, u32[]{:S(2)}) async-start(bf16[4,336,512]{2,1,0:T(8,128)(2,1)} %bitcast.76), calls=%async_computation | async-start | bytes 2752512 | tf_op jit(solution)/shard_map/all_to_all | solution.py:182
  9.6 1.6 %fusion.3 = bf16[16,1536]{1,0:T(8,128)(2,1)S(1)} fusion(s32[1344]{0:T(1024)S(1)} %copy-done.9, bf16[16,1280]{1,0:T(8,128)(2,1)S(1)} %reshape.159), kind=kOutput, calls=%fused_computation.5 | convolution fusion | flops 68149248 | bytes 95488 | tf_op jit(solution)/shard_map/dot_general | solution.py:179
  11.2 0.2 reshape.160
  11.4 0.1 copy.24
  11.4 0.2 reshape.161.hidden_ref
  12.3 0.3 fusion.8
  12.6 1.4 %fusion.30 = (f32[4,5]{1,0:T(4,128)S(1)}, f32[4,5,2048]{2,1,0:T(8,128)S(1)}) fusion(bf16[4,5,128]{2,1,0:T(8,128)(2,1)S(1)} %reshape.163, bf16[1,2048,128]{2,1,0:T(8,128)(2,1)} %param.23, pred[2048]{0:T(1024)(128)(4,1)S(1)} %iota_compare_fusion.4), kind=kOutput, calls=%fused_computation.50 | convolution fusion | flops 10608620 | bytes 695376 | tf_op jit(solution)/shard_map/rsgqd,rcgd->rgsqc/dot_general | solution.py:27
  14.0 7.1 %all-to-all-done = bf16[4,336,512]{2,1,0:T(8,128)(2,1)S(1)} async-done(((bf16[4,336,512]{2,1,0:T(8,128)(2,1)}), bf16[4,336,512]{2,1,0:T(8,128)(2,1)S(1)}, u32[]{:S(2)}, u32[]{:S(2)}) %all-to-all-start) | async-done | bytes 1376288 | tf_op jit(solution)/shard_map/all_to_all | solution.py:182
  21.1 0.6 blocks.1
  21.7 43.9 %all_to_all.38 = bf16[48,8,512]{2,1,0:T(8,128)(2,1)S(1)} all-to-all(bf16[48,8,512]{2,1,0:T(8,128)(2,1)S(1)} %bitcast.75), channel_id=1, replica_groups=mesh['x'=4,'y'=4,'z'=12,'h'=2,'c'=2] {'z','y'}, dimensions={0} | all-to-all | bytes 786432 | tf_op jit(solution)/shard_map/all_to_all | solution.py:200
  65.6 0.1 convert_reduce_fusion
  65.8 0.7 fusion.28
  66.5 0.3 slice_reduce_fusion
  66.8 17.6 %all_to_all.39 = bf16[16,8,128]{2,1,0:T(8,128)(2,1)S(1)} all-to-all(bf16[16,8,128]{2,1,0:T(8,128)(2,1)S(1)} %bitcast.81), channel_id=1, replica_groups=mesh['x'=4,'y'=4,'z'=12,'h'=2,'c'=2] {'h','c','x'}, dimensions={0} | all-to-all | bytes 65536 | tf_op jit(solution)/shard_map/all_to_all | solution.py:216
  84.4 0.1 fusion.14
  84.6 16.3 %all_to_all.40 = f32[48,4,128]{2,1,0:T(4,128)S(1)} all-to-all(f32[48,4,128]{2,1,0:T(4,128)S(1)} %copy.26), channel_id=1, replica_groups=mesh['x'=4,'y'=4,'z'=12,'h'=2,'c'=2] {'z','y'}, dimensions={0} | all-to-all | bytes 196608 | tf_op jit(solution)/shard_map/all_to_all | solution.py:218
  100.9 0.1 reduce_sum.40
  101.0 0.2 fusion.31
  101.2 0.2 fusion.11
  101.4 0.3 convolution_bitcast_fusion
  101.7 0.2 fusion.5
  101.9 0.6 reshape.171
  (31 shorter events, 0.2 us)
Async XLA Ops:
  0.6 11.7 %copy-start = (bf16[5120,128]{1,0:T(8,128)(2,1)S(1)}, bf16[5120,128]{1,0:T(8,128)(2,1)}, u32[]{:S(2)}) copy-start(bf16[5120,128]{1,0:T(8,128)(2,1)} %param.26) | copy-start | bytes 3932164
  4.6 5.0 %copy-start.1 = (bf16[1,4,5120]{2,1,0:T(4,128)(2,1)S(1)}, bf16[1,4,5120]{2,1,0:T(4,128)(2,1)}, u32[]{:S(2)}) copy-start(bf16[1,4,5120]{2,1,0:T(4,128)(2,1)} %param.21) | copy-start | bytes 122884
  4.6 5.0 %copy-start.9 = (s32[1344]{0:T(1024)S(1)}, s32[1344]{0:T(1024)}, u32[]{:S(2)}) copy-start(s32[1344]{0:T(1024)} %constant.30.clone) | copy-start | bytes 16132
  4.6 16.5 %all-to-all-start = ((bf16[4,336,512]{2,1,0:T(8,128)(2,1)}), bf16[4,336,512]{2,1,0:T(8,128)(2,1)S(1)}, u32[]{:S(2)}, u32[]{:S(2)}) async-start(bf16[4,336,512]{2,1,0:T(8,128)(2,1)} %bitcast.76), calls=%async_computation | async-start | bytes 2752512 | tf_op jit(solution)/shard_map/all_to_all | solution.py:182
  9.6 2.0 %copy-start.5 = (bf16[1,4,640]{2,1,0:T(4,128)(2,1)S(1)}, bf16[1,4,640]{2,1,0:T(4,128)(2,1)}, u32[]{:S(2)}) copy-start(bf16[1,4,640]{2,1,0:T(4,128)(2,1)} %param.22) | copy-start | bytes 15364
  12.6 89.1 %copy-start.6 = (bf16[1,4,128]{2,1,0:T(4,128)(2,1)}, bf16[1,4,128]{2,1,0:T(4,128)(2,1)S(1)}, u32[]{:S(2)}) copy-start(bf16[1,4,128]{2,1,0:T(4,128)(2,1)S(1)} %fusion.8) | copy-start | bytes 3076
  21.1 44.7 %copy-start.2 = (f32[1,7,512]{2,0,1:T(1,128)S(1)}, f32[1,7,512]{2,0,1:T(1,128)}, u32[]{:S(2)}) copy-start(f32[1,7,512]{2,0,1:T(1,128)} %param.18) | copy-start | bytes 43012
  21.1 44.7 %copy-start.3 = (f32[1,7,512]{2,0,1:T(1,128)S(1)}, f32[1,7,512]{2,0,1:T(1,128)}, u32[]{:S(2)}) copy-start(f32[1,7,512]{2,0,1:T(1,128)} %param.19) | copy-start | bytes 43012
  21.1 44.7 %copy-start.4 = (f32[1,7,512]{2,0,1:T(1,128)S(1)}, f32[1,7,512]{2,0,1:T(1,128)}, u32[]{:S(2)}) copy-start(f32[1,7,512]{2,0,1:T(1,128)} %param.20) | copy-start | bytes 43012
  21.7 79.7 %copy-start.8 = (bf16[1,2048,128]{2,1,0:T(8,128)(2,1)S(1)}, bf16[1,2048,128]{2,1,0:T(8,128)(2,1)}, u32[]{:S(2)}) copy-start(bf16[1,2048,128]{2,1,0:T(8,128)(2,1)} %param.24) | copy-start | bytes 1572868
  101.0 1.6 %copy-start.7 = (bf16[4,128]{1,0:T(4,128)(2,1)}, bf16[4,128]{1,0:T(4,128)(2,1)S(1)}, u32[]{:S(2)}) copy-start(bf16[4,128]{1,0:T(4,128)(2,1)S(1)} %reduce_sum.40) | copy-start | bytes 3076

commit v7 on v6

--- a/solution.py
+++ b/solution.py
@@ -62,25 +62,9 @@
     return (jnp.asarray(target, jnp.int32)[:, None] == c).astype(jnp.bfloat16)
 
 
-def gradient_kernel(
-    len_ref, adv_ref, act_hbm, cot_hbm, out_hbm, act_ref, cot_ref, wgt_ref, out_ref, sem
-):
+def gradient_kernel(len_ref, adv_ref, act_ref, cot_ref, out_hbm, wgt_ref, out_ref, sem):
     tok_rows, quarter_rows = act_ref.shape
     parts = quarter_rows // CHUNK
-    cot_in = pltpu.make_async_copy(cot_hbm, cot_ref, sem.at[0])
-    cot_in.start()
-    loads, stores = [], []
-    for i in range(parts):
-        cols = pl.ds(i * CHUNK, CHUNK)
-        loads.append(
-            pltpu.make_async_copy(act_hbm.at[:, cols], act_ref.at[:, cols], sem.at[1 + i])
-        )
-        loads[i].start()
-        end = (i + 1) * CHUNK if i + 1 < parts else out_ref.shape[0]
-        rows = pl.ds(i * CHUNK, end - i * CHUNK)
-        stores.append(
-            pltpu.make_async_copy(out_ref.at[rows], out_hbm.at[rows], sem.at[1 + parts + i])
-        )
     rest = out_ref.shape[0] - quarter_rows
     out_ref[quarter_rows:, :] = jnp.zeros((rest, out_ref.shape[1]), jnp.bfloat16)
     group = lax.axis_index(("x", "y", "z"))
@@ -88,18 +72,20 @@
     adv = adv_ref[group].astype(jnp.float32)
     within = lax.broadcasted_iota(jnp.int32, (tok_rows, HD), 0)
     scale = jnp.where(within < length, adv / 256.0, jnp.float32(0.0)) / len_ref.shape[0]
-    cot_in.wait()
     for c in range(cot_ref.shape[1] // HD):
         cols = pl.ds(c * HD, HD)
         wgt_ref[:, cols] = (cot_ref[:, cols].astype(jnp.float32) * scale).astype(jnp.bfloat16)
+    stores = []
     for i in range(parts):
-        loads[i].wait()
         out_ref[i * CHUNK : (i + 1) * CHUNK, :] = lax.dot_general(
             act_ref[:, i * CHUNK : (i + 1) * CHUNK],
             wgt_ref[...],
             (((0,), (0,)), ((), ())),
             preferred_element_type=jnp.float32,
         ).astype(jnp.bfloat16)
+        end = (i + 1) * CHUNK if i + 1 < parts else out_ref.shape[0]
+        rows = pl.ds(i * CHUNK, end - i * CHUNK)
+        stores.append(pltpu.make_async_copy(out_ref.at[rows], out_hbm.at[rows], sem.at[i]))
         stores[i].start()
     for i in range(parts):
         stores[i].wait()
@@ -148,19 +134,16 @@
     width = cotangent.shape[1]
     smem = pl.BlockSpec(memory_space=pltpu.SMEM)
     vmem = pl.BlockSpec(memory_space=pltpu.VMEM)
-    hbm = pl.BlockSpec(memory_space=pl.ANY)
     small = pltpu.CompilerParams(vmem_limit_bytes=16 * 2**20)
     partial = pl.pallas_call(
         gradient_kernel,
         out_shape=jax.ShapeDtypeStruct((padded_rows, width), bf16),
-        in_specs=[smem, smem, hbm, hbm],
-        out_specs=hbm,
+        in_specs=[smem, smem, vmem, vmem],
+        out_specs=pl.BlockSpec(memory_space=pl.ANY),
         scratch_shapes=[
-            pltpu.VMEM((tok_rows, quarter_rows), bf16),
-            pltpu.VMEM((tok_rows, width), bf16),
             pltpu.VMEM((tok_rows, width), bf16),
             pltpu.VMEM((padded_rows, width), bf16),
-            pltpu.SemaphoreType.DMA((1 + 2 * (quarter_rows // CHUNK),)),
+            pltpu.SemaphoreType.DMA((quarter_rows // CHUNK,)),
         ],
         name="gradient",
     )(seq_len, advantage, activations, cotangent)

time: 103 us -> 102 us (level)
  Pallas kernels: 4.51 us -> 3.29 us
    pallas_call x1, Pallas kernels: 3.93 us -> 2.71 us  [shards(): pl.pallas_call(gradient_kernel, out_shape=jax.ShapeDtypeStruct((padded_ro...]
where the time goes in v7:
time: 102 us; the launch traced here: 101 us
  blocking collectives  77.8 us (76%)
  waiting for transfers between devices  7.07 us (7%)
  starting transfers between devices  4.98 us (5%)
  matrix products  4 us (4%)
  Pallas kernels  3.29 us (3%)
  local copies, waits for them, and re-layouts  1.53 us (2%)
  between operations  1.49 us (1%)
  other arithmetic  1.12 us (1%)
    all_to_all x1, blocking collectives, shards(): lax.all_to_all(part_x, ('z', 'y'), 0, 0, tiled=True)  43.9 us
    all_to_all x1, blocking collectives, shards(): weight = lax.all_to_all(send, ('h', 'c', 'x'), 0, 0, tiled=True)  17.6 us
    all_to_all x1, blocking collectives, shards(): lax.all_to_all(keys_yz.reshape(blocks, steps, HD), ('z', 'y'), 0, 0, tile...  16.3 us
    all_to_all x1, waiting for transfers between devices, shards(): got = lax.all_to_all(partial, 'x', 0, 0, tiled=True)  7.07 us
    all_to_all x1, starting transfers between devices, shards(): got = lax.all_to_all(partial, 'x', 0, 0, tiled=True)  4.98 us
    pallas_call x1, Pallas kernels, shards(): pl.pallas_call(gradient_kernel, out_shape=jax.ShapeDtypeStruct((padded_ro...  2.71 us
  transfers between devices with their start and end apart: 1, of which 1 were waited for; matrix products, arithmetic and copies ran while one was open for 4% of the time, Pallas kernels for 0%

profile of v7, /device:TPU:1, one launch (start us, length us, event | category | flops | bytes accessed | tf_op | source)
XLA Modules:
  0.0 101.3 jit_solution(423226141637545942)
XLA Ops:
  0.6 0.0 copy-start
  0.6 2.7 %gradient.1 = bf16[1344,512]{1,0:T(8,128)(2,1)} custom-call(s32[192]{0:T(256)} %len_ref.1, s32[192]{0:T(256)} %adv_ref.1, bf16[256,1280]{1,0:T(8,128)(2,1)} %act_ref.1, bf16[256,512]{1,0:T(8,128)(2,1)} %cot_ref.1), custom_call_target="tpu_custom_call" | custom-call | tf_op jit(solution)/shard_map/gradient/pallas_call | solution.py:138
  3.4 5.0 %all-to-all-start = ((bf16[4,336,512]{2,1,0:T(8,128)(2,1)}), bf16[4,336,512]{2,1,0:T(8,128)(2,1)S(1)}, u32[]{:S(2)}, u32[]{:S(2)}) async-start(bf16[4,336,512]{2,1,0:T(8,128)(2,1)} %bitcast.76), calls=%async_computation | async-start | bytes 2752512 | tf_op jit(solution)/shard_map/all_to_all | solution.py:165
  8.4 1.6 %fusion.3 = bf16[16,1536]{1,0:T(8,128)(2,1)S(1)} fusion(s32[1344]{0:T(1024)S(1)} %copy-done.9, bf16[16,1280]{1,0:T(8,128)(2,1)S(1)} %reshape.159), kind=kOutput, calls=%fused_computation.5 | convolution fusion | flops 68149248 | bytes 95488 | tf_op jit(solution)/shard_map/dot_general | solution.py:162
  10.0 0.2 reshape.160
  10.2 0.1 copy.24
  10.2 0.2 reshape.161.hidden_ref
  11.1 0.3 fusion.8
  11.4 1.4 %fusion.30 = (f32[4,5]{1,0:T(4,128)S(1)}, f32[4,5,2048]{2,1,0:T(8,128)S(1)}) fusion(bf16[4,5,128]{2,1,0:T(8,128)(2,1)S(1)} %reshape.163, bf16[1,2048,128]{2,1,0:T(8,128)(2,1)} %param.23, pred[2048]{0:T(1024)(128)(4,1)S(1)} %iota_compare_fusion.4), kind=kOutput, calls=%fused_computation.50 | convolution fusion | flops 10608620 | bytes 695376 | tf_op jit(solution)/shard_map/rsgqd,rcgd->rgsqc/dot_general | solution.py:27
  12.8 7.1 %all-to-all-done = bf16[4,336,512]{2,1,0:T(8,128)(2,1)S(1)} async-done(((bf16[4,336,512]{2,1,0:T(8,128)(2,1)}), bf16[4,336,512]{2,1,0:T(8,128)(2,1)S(1)}, u32[]{:S(2)}, u32[]{:S(2)}) %all-to-all-start) | async-done | bytes 1376288 | tf_op jit(solution)/shard_map/all_to_all | solution.py:165
  19.9 0.6 blocks.1
  20.5 43.9 %all_to_all.38 = bf16[48,8,512]{2,1,0:T(8,128)(2,1)S(1)} all-to-all(bf16[48,8,512]{2,1,0:T(8,128)(2,1)S(1)} %bitcast.75), channel_id=1, replica_groups=mesh['x'=4,'y'=4,'z'=12,'h'=2,'c'=2] {'z','y'}, dimensions={0} | all-to-all | bytes 786432 | tf_op jit(solution)/shard_map/all_to_all | solution.py:183
  64.4 0.1 convert_reduce_fusion
  64.5 0.7 fusion.28
  65.3 0.3 slice_reduce_fusion
  65.6 17.6 %all_to_all.39 = bf16[16,8,128]{2,1,0:T(8,128)(2,1)S(1)} all-to-all(bf16[16,8,128]{2,1,0:T(8,128)(2,1)S(1)} %bitcast.81), channel_id=1, replica_groups=mesh['x'=4,'y'=4,'z'=12,'h'=2,'c'=2] {'h','c','x'}, dimensions={0} | all-to-all | bytes 65536 | tf_op jit(solution)/shard_map/all_to_all | solution.py:199
  83.2 0.1 fusion.14
  83.4 16.3 %all_to_all.40 = f32[48,4,128]{2,1,0:T(4,128)S(1)} all-to-all(f32[48,4,128]{2,1,0:T(4,128)S(1)} %copy.26), channel_id=1, replica_groups=mesh['x'=4,'y'=4,'z'=12,'h'=2,'c'=2] {'z','y'}, dimensions={0} | all-to-all | bytes 196608 | tf_op jit(solution)/shard_map/all_to_all | solution.py:201
  99.7 0.1 reduce_sum.40
  99.8 0.2 fusion.31
  99.9 0.2 fusion.11
  100.2 0.3 convolution_bitcast_fusion
  100.5 0.2 fusion.5
  100.7 0.6 reshape.171
  (31 shorter events, 0.2 us)
Async XLA Ops:
  0.6 10.5 %copy-start = (bf16[5120,128]{1,0:T(8,128)(2,1)S(1)}, bf16[5120,128]{1,0:T(8,128)(2,1)}, u32[]{:S(2)}) copy-start(bf16[5120,128]{1,0:T(8,128)(2,1)} %param.26) | copy-start | bytes 3932164
  3.4 5.0 %copy-start.1 = (bf16[1,4,5120]{2,1,0:T(4,128)(2,1)S(1)}, bf16[1,4,5120]{2,1,0:T(4,128)(2,1)}, u32[]{:S(2)}) copy-start(bf16[1,4,5120]{2,1,0:T(4,128)(2,1)} %param.21) | copy-start | bytes 122884
  3.4 5.0 %copy-start.9 = (s32[1344]{0:T(1024)S(1)}, s32[1344]{0:T(1024)}, u32[]{:S(2)}) copy-start(s32[1344]{0:T(1024)} %constant.30.clone) | copy-start | bytes 16132
  3.4 16.5 %all-to-all-start = ((bf16[4,336,512]{2,1,0:T(8,128)(2,1)}), bf16[4,336,512]{2,1,0:T(8,128)(2,1)S(1)}, u32[]{:S(2)}, u32[]{:S(2)}) async-start(bf16[4,336,512]{2,1,0:T(8,128)(2,1)} %bitcast.76), calls=%async_computation | async-start | bytes 2752512 | tf_op jit(solution)/shard_map/all_to_all | solution.py:165
  8.4 2.0 %copy-start.5 = (bf16[1,4,640]{2,1,0:T(4,128)(2,1)S(1)}, bf16[1,4,640]{2,1,0:T(4,128)(2,1)}, u32[]{:S(2)}) copy-start(bf16[1,4,640]{2,1,0:T(4,128)(2,1)} %param.22) | copy-start | bytes 15364
  11.4 89.1 %copy-start.6 = (bf16[1,4,128]{2,1,0:T(4,128)(2,1)}, bf16[1,4,128]{2,1,0:T(4,128)(2,1)S(1)}, u32[]{:S(2)}) copy-start(bf16[1,4,128]{2,1,0:T(4,128)(2,1)S(1)} %fusion.8) | copy-start | bytes 3076
  19.9 44.7 %copy-start.2 = (f32[1,7,512]{2,0,1:T(1,128)S(1)}, f32[1,7,512]{2,0,1:T(1,128)}, u32[]{:S(2)}) copy-start(f32[1,7,512]{2,0,1:T(1,128)} %param.18) | copy-start | bytes 43012
  19.9 44.7 %copy-start.3 = (f32[1,7,512]{2,0,1:T(1,128)S(1)}, f32[1,7,512]{2,0,1:T(1,128)}, u32[]{:S(2)}) copy-start(f32[1,7,512]{2,0,1:T(1,128)} %param.19) | copy-start | bytes 43012
  19.9 44.7 %copy-start.4 = (f32[1,7,512]{2,0,1:T(1,128)S(1)}, f32[1,7,512]{2,0,1:T(1,128)}, u32[]{:S(2)}) copy-start(f32[1,7,512]{2,0,1:T(1,128)} %param.20) | copy-start | bytes 43012
  20.5 79.7 %copy-start.8 = (bf16[1,2048,128]{2,1,0:T(8,128)(2,1)S(1)}, bf16[1,2048,128]{2,1,0:T(8,128)(2,1)}, u32[]{:S(2)}) copy-start(bf16[1,2048,128]{2,1,0:T(8,128)(2,1)} %param.24) | copy-start | bytes 1572868
  99.8 1.6 %copy-start.7 = (bf16[4,128]{1,0:T(4,128)(2,1)}, bf16[4,128]{1,0:T(4,128)(2,1)S(1)}, u32[]{:S(2)}) copy-start(bf16[4,128]{1,0:T(4,128)(2,1)S(1)} %reduce_sum.40) | copy-start | bytes 3076

commit v8 on v7

--- a/solution.py
+++ b/solution.py
@@ -194,9 +194,10 @@
     relay = jnp.pad(master_new[0].astype(bf16), ((0, PAD - OWN), (0, 0)))
 
     heads = relay.reshape(PAD, TP, HD).transpose(1, 0, 2)
-    send = jnp.broadcast_to(heads[:, None], (TP, NX, PAD, HD)).reshape(-1, HD)
+    send = jnp.broadcast_to(heads[None], (NX, TP, PAD, HD)).reshape(-1, HD)
     send, hidden_yz = lax.optimization_barrier((send, hidden_yz))
-    weight = lax.all_to_all(send, ("h", "c", "x"), 0, 0, tiled=True)
+    got = lax.all_to_all(send, ("x", "h", "c"), 0, 0, tiled=True)
+    weight = got.reshape(NX, TP, PAD, HD).transpose(1, 0, 2, 3).reshape(-1, HD)
     keys_yz = jnp.dot(hidden_yz, weight, preferred_element_type=f32)
     got = lax.all_to_all(keys_yz.reshape(blocks, steps, HD), ("z", "y"), 0, 0, tiled=True)
     new_keys = jnp.sum(got, axis=0).astype(bf16)[None]

time: 102 us -> 102 us (level)
  no operation moved by 1% of the time
where the time goes in v8:
time: 102 us; the launch traced here: 101 us
  blocking collectives  77.8 us (76%)
  waiting for transfers between devices  7.07 us (7%)
  starting transfers between devices  4.98 us (5%)
  matrix products  4.01 us (4%)
  Pallas kernels  3.29 us (3%)
  local copies, waits for them, and re-layouts  1.53 us (2%)
  between operations  1.49 us (1%)
  other arithmetic  1.12 us (1%)
    all_to_all x1, blocking collectives, shards(): lax.all_to_all(part_x, ('z', 'y'), 0, 0, tiled=True)  43.9 us
    all_to_all x1, blocking collectives, shards(): got = lax.all_to_all(send, ('x', 'h', 'c'), 0, 0, tiled=True)  17.6 us
    all_to_all x1, blocking collectives, shards(): lax.all_to_all(keys_yz.reshape(blocks, steps, HD), ('z', 'y'), 0, 0, tile...  16.3 us
    all_to_all x1, waiting for transfers between devices, shards(): got = lax.all_to_all(partial, 'x', 0, 0, tiled=True)  7.07 us
    all_to_all x1, starting transfers between devices, shards(): got = lax.all_to_all(partial, 'x', 0, 0, tiled=True)  4.98 us
    pallas_call x1, Pallas kernels, shards(): pl.pallas_call(gradient_kernel, out_shape=jax.ShapeDtypeStruct((padded_ro...  2.71 us
  transfers between devices with their start and end apart: 1, of which 1 were waited for; matrix products, arithmetic and copies ran while one was open for 4% of the time, Pallas kernels for 0%

profile of v8, /device:TPU:1, one launch (start us, length us, event | category | flops | bytes accessed | tf_op | source)
XLA Modules:
  0.0 101.3 jit_solution(16301047863623011724)
XLA Ops:
  0.6 0.0 copy-start
  0.6 2.7 %gradient.1 = bf16[1344,512]{1,0:T(8,128)(2,1)} custom-call(s32[192]{0:T(256)} %len_ref.1, s32[192]{0:T(256)} %adv_ref.1, bf16[256,1280]{1,0:T(8,128)(2,1)} %act_ref.1, bf16[256,512]{1,0:T(8,128)(2,1)} %cot_ref.1), custom_call_target="tpu_custom_call" | custom-call | tf_op jit(solution)/shard_map/gradient/pallas_call | solution.py:138
  3.4 5.0 %all-to-all-start = ((bf16[4,336,512]{2,1,0:T(8,128)(2,1)}), bf16[4,336,512]{2,1,0:T(8,128)(2,1)S(1)}, u32[]{:S(2)}, u32[]{:S(2)}) async-start(bf16[4,336,512]{2,1,0:T(8,128)(2,1)} %bitcast.78), calls=%async_computation | async-start | bytes 2752512 | tf_op jit(solution)/shard_map/all_to_all | solution.py:165
  8.4 1.6 %fusion.3 = bf16[16,1536]{1,0:T(8,128)(2,1)S(1)} fusion(s32[1344]{0:T(1024)S(1)} %copy-done.9, bf16[16,1280]{1,0:T(8,128)(2,1)S(1)} %reshape.166), kind=kOutput, calls=%fused_computation.5 | convolution fusion | flops 68149248 | bytes 95488 | tf_op jit(solution)/shard_map/dot_general | solution.py:162
  10.0 0.2 reshape.167
  10.2 0.1 copy.25
  10.2 0.2 reshape.168.hidden_ref
  11.1 0.3 fusion.8
  11.4 1.4 %fusion.29 = (f32[4,5]{1,0:T(4,128)S(1)}, f32[4,5,2048]{2,1,0:T(8,128)S(1)}) fusion(bf16[4,5,128]{2,1,0:T(8,128)(2,1)S(1)} %reshape.170, bf16[1,2048,128]{2,1,0:T(8,128)(2,1)} %param.23, pred[2048]{0:T(1024)(128)(4,1)S(1)} %iota_compare_fusion.4), kind=kOutput, calls=%fused_computation.49 | convolution fusion | flops 10608620 | bytes 695376 | tf_op jit(solution)/shard_map/rsgqd,rcgd->rgsqc/dot_general | solution.py:27
  12.8 7.1 %all-to-all-done = bf16[4,336,512]{2,1,0:T(8,128)(2,1)S(1)} async-done(((bf16[4,336,512]{2,1,0:T(8,128)(2,1)}), bf16[4,336,512]{2,1,0:T(8,128)(2,1)S(1)}, u32[]{:S(2)}, u32[]{:S(2)}) %all-to-all-start) | async-done | bytes 1376288 | tf_op jit(solution)/shard_map/all_to_all | solution.py:165
  19.9 0.6 blocks.1
  20.5 43.9 %all_to_all.35 = bf16[48,8,512]{2,1,0:T(8,128)(2,1)S(1)} all-to-all(bf16[48,8,512]{2,1,0:T(8,128)(2,1)S(1)} %bitcast.77), channel_id=1, replica_groups=mesh['x'=4,'y'=4,'z'=12,'h'=2,'c'=2] {'z','y'}, dimensions={0} | all-to-all | bytes 786432 | tf_op jit(solution)/shard_map/all_to_all | solution.py:183
  64.4 0.1 convert_reduce_fusion
  64.5 0.7 fusion.27
  65.3 0.3 slice_reduce_fusion
  65.6 17.6 %all_to_all.36 = bf16[16,8,128]{2,1,0:T(8,128)(2,1)S(1)} all-to-all(bf16[16,8,128]{2,1,0:T(8,128)(2,1)S(1)} %bitcast.83), channel_id=1, replica_groups=mesh['x'=4,'y'=4,'z'=12,'h'=2,'c'=2] {'x','h','c'}, dimensions={0} | all-to-all | bytes 65536 | tf_op jit(solution)/shard_map/all_to_all | solution.py:199
  83.2 0.1 fusion.14
  83.4 16.3 %all_to_all.37 = f32[48,4,128]{2,1,0:T(4,128)S(1)} all-to-all(f32[48,4,128]{2,1,0:T(4,128)S(1)} %copy.28), channel_id=1, replica_groups=mesh['x'=4,'y'=4,'z'=12,'h'=2,'c'=2] {'z','y'}, dimensions={0} | all-to-all | bytes 196608 | tf_op jit(solution)/shard_map/all_to_all | solution.py:202
  99.7 0.1 reduce_sum.40
  99.8 0.2 fusion.30
  99.9 0.2 fusion.11
  100.2 0.3 convolution_bitcast_fusion
  100.5 0.2 fusion.5
  100.7 0.6 reshape.180
  (32 shorter events, 0.3 us)
Async XLA Ops:
  0.6 10.5 %copy-start = (bf16[5120,128]{1,0:T(8,128)(2,1)S(1)}, bf16[5120,128]{1,0:T(8,128)(2,1)}, u32[]{:S(2)}) copy-start(bf16[5120,128]{1,0:T(8,128)(2,1)} %param.26) | copy-start | bytes 3932164
  3.4 5.0 %copy-start.1 = (bf16[1,4,5120]{2,1,0:T(4,128)(2,1)S(1)}, bf16[1,4,5120]{2,1,0:T(4,128)(2,1)}, u32[]{:S(2)}) copy-start(bf16[1,4,5120]{2,1,0:T(4,128)(2,1)} %param.21) | copy-start | bytes 122884
  3.4 5.0 %copy-start.9 = (s32[1344]{0:T(1024)S(1)}, s32[1344]{0:T(1024)}, u32[]{:S(2)}) copy-start(s32[1344]{0:T(1024)} %constant.30.clone) | copy-start | bytes 16132
  3.4 16.5 %all-to-all-start = ((bf16[4,336,512]{2,1,0:T(8,128)(2,1)}), bf16[4,336,512]{2,1,0:T(8,128)(2,1)S(1)}, u32[]{:S(2)}, u32[]{:S(2)}) async-start(bf16[4,336,512]{2,1,0:T(8,128)(2,1)} %bitcast.78), calls=%async_computation | async-start | bytes 2752512 | tf_op jit(solution)/shard_map/all_to_all | solution.py:165
  8.4 2.0 %copy-start.5 = (bf16[1,4,640]{2,1,0:T(4,128)(2,1)S(1)}, bf16[1,4,640]{2,1,0:T(4,128)(2,1)}, u32[]{:S(2)}) copy-start(bf16[1,4,640]{2,1,0:T(4,128)(2,1)} %param.22) | copy-start | bytes 15364
  11.4 89.1 %copy-start.6 = (bf16[1,4,128]{2,1,0:T(4,128)(2,1)}, bf16[1,4,128]{2,1,0:T(4,128)(2,1)S(1)}, u32[]{:S(2)}) copy-start(bf16[1,4,128]{2,1,0:T(4,128)(2,1)S(1)} %fusion.8) | copy-start | bytes 3076
  19.9 44.7 %copy-start.2 = (f32[1,7,512]{2,0,1:T(1,128)S(1)}, f32[1,7,512]{2,0,1:T(1,128)}, u32[]{:S(2)}) copy-start(f32[1,7,512]{2,0,1:T(1,128)} %param.18) | copy-start | bytes 43012
  19.9 44.7 %copy-start.3 = (f32[1,7,512]{2,0,1:T(1,128)S(1)}, f32[1,7,512]{2,0,1:T(1,128)}, u32[]{:S(2)}) copy-start(f32[1,7,512]{2,0,1:T(1,128)} %param.19) | copy-start | bytes 43012
  19.9 44.7 %copy-start.4 = (f32[1,7,512]{2,0,1:T(1,128)S(1)}, f32[1,7,512]{2,0,1:T(1,128)}, u32[]{:S(2)}) copy-start(f32[1,7,512]{2,0,1:T(1,128)} %param.20) | copy-start | bytes 43012
  20.5 79.7 %copy-start.8 = (bf16[1,2048,128]{2,1,0:T(8,128)(2,1)S(1)}, bf16[1,2048,128]{2,1,0:T(8,128)(2,1)}, u32[]{:S(2)}) copy-start(bf16[1,2048,128]{2,1,0:T(8,128)(2,1)} %param.24) | copy-start | bytes 1572868
  99.8 1.6 %copy-start.7 = (bf16[4,128]{1,0:T(4,128)(2,1)}, bf16[4,128]{1,0:T(4,128)(2,1)S(1)}, u32[]{:S(2)}) copy-start(bf16[4,128]{1,0:T(4,128)(2,1)S(1)} %reduce_sum.40) | copy-start | bytes 3076
